TPU v7x, 512 devices: a whole 4x4x16 slice. The times are simulated.
512 devices in a mesh: seq: 64 (over y, z), req: 8 (over x, core).
Axes of the slice: x: 4, y: 4, z: 16, core: 2. Of those that a mesh axis runs over, the one named last changes fastest.
Arguments:
- new_token_queries: bfloat16 [4, 64, 2048], P(None, 'req'), may hold values from -48 to 48
- new_token_keys: bfloat16 [4, 64, 1024], P(None, 'req'), may hold values from -48 to 48
- new_token_values: bfloat16 [4, 64, 1024], P(None, 'req'), may hold values from -6 to 6
- key_cache: bfloat16 [64, 2048, 1024], P('req', 'seq'), may hold values from -48 to 48
- value_cache: bfloat16 [64, 2048, 1024], P('req', 'seq'), may hold values from -6 to 6
- cache_len: int32 [64], P('req'), may hold values from 1 to 2048, 34816 in all
- resid: bfloat16 [4, 64, 2048], P(None, 'req'), may hold values from -6 to 6
- gain: bfloat16 [2048], replicated, may hold values from 0.5 to 1.5
- w_gate: bfloat16 [2048, 6144], P('seq', 'req'), may hold values from -0.125 to 0.125
- w_up: bfloat16 [2048, 6144], P('seq', 'req'), may hold values from -0.125 to 0.125
- w_down: bfloat16 [6144, 2048], P('req', 'seq'), may hold values from -0.078125 to 0.078125
Outputs:
- out: bfloat16 [4, 64, 2048], P(None, 'req')
All inputs are finite; a program needn't handle non-finite values. No bound on the sum of `cache_len` on one device may be relied on, other than what follows from the above.
Results may differ from a plain program's by a relative error of at most 0.006.
Values may be sent and summed in bfloat16 or wider, within the bound.
A program may use at most 128 MiB of HBM per device.

v0:
```python
import math

import jax
import jax.numpy as jnp
from jax import lax
from jax.sharding import PartitionSpec as P

QUERY_HEADS = 16
KEY_VALUE_HEADS = 8
HEAD_SIZE = 128
DECODE_STEPS = 4


NEG_FILL = -1e30
EPSILON = 1e-06


def page_partial(query_vector, key_row_set, value_row_set, valid):
    scores = jnp.einsum(
        "rkgd,rbkd->rkgb", query_vector, key_row_set, preferred_element_type=jnp.float32
    ) / math.sqrt(HEAD_SIZE)
    inside = valid[:, None, None, :]
    scores = jnp.where(inside, scores, NEG_FILL)
    highest = jnp.max(scores, axis=-1)
    weights = jnp.where(inside, jnp.exp(scores - highest[..., None]), 0.0).astype(jnp.bfloat16)
    totals = jnp.sum(weights.astype(jnp.float32), axis=-1)
    weighted = jnp.einsum(
        "rkgb,rbkd->rkgd", weights, value_row_set, preferred_element_type=jnp.float32
    )
    return (highest, totals, weighted)


def merge_pair(former, latter):
    highest = jnp.maximum(former[0], latter[0])
    first_scale = jnp.exp(former[0] - highest)
    second_scale = jnp.exp(latter[0] - highest)
    totals = first_scale * former[1] + second_scale * latter[1]
    weighted = first_scale[..., None] * former[2] + second_scale[..., None] * latter[2]
    return (highest, totals, weighted)


def body(
    new_token_queries,
    new_token_keys,
    new_token_values,
    key_cache,
    value_cache,
    cache_len,
    resid,
    gain,
    w_gate,
    w_up,
    w_down,
):
    count_of_rows = new_token_queries.shape[1]
    page_length = key_cache.shape[1]
    head_cluster = QUERY_HEADS // KEY_VALUE_HEADS
    slice_width = w_gate.shape[0]
    unit_count = w_gate.shape[1]
    seq_index = lax.axis_index("seq")
    positions = seq_index * page_length + jnp.arange(page_length, dtype=jnp.int32)
    valid = positions[None, :] < cache_len[:, None]
    key_row_set = key_cache.reshape(count_of_rows, page_length, KEY_VALUE_HEADS, HEAD_SIZE)
    value_row_set = value_cache.reshape(count_of_rows, page_length, KEY_VALUE_HEADS, HEAD_SIZE)
    joined = jnp.concatenate([w_gate, w_up], axis=1)
    gain_scale = gain.astype(jnp.float32)
    results = []
    for decode_step_index in range(DECODE_STEPS):
        query_vector = new_token_queries[decode_step_index].reshape(
            count_of_rows, KEY_VALUE_HEADS, head_cluster, HEAD_SIZE
        )
        local = page_partial(query_vector, key_row_set, value_row_set, valid)
        highest = lax.pmax(local[0], "seq")
        factor = jnp.exp(local[0] - highest)
        totals, weighted = lax.psum((factor * local[1], factor[..., None] * local[2]), "seq")
        incoming_keys = jnp.swapaxes(new_token_keys[: decode_step_index + 1], 0, 1).reshape(
            count_of_rows, decode_step_index + 1, KEY_VALUE_HEADS, HEAD_SIZE
        )
        incoming_values = jnp.swapaxes(new_token_values[: decode_step_index + 1], 0, 1).reshape(
            count_of_rows, decode_step_index + 1, KEY_VALUE_HEADS, HEAD_SIZE
        )
        fresh_valid = jnp.ones((count_of_rows, decode_step_index + 1), jnp.bool_)
        fresh = page_partial(query_vector, incoming_keys, incoming_values, fresh_valid)
        combined = merge_pair((highest, totals, weighted), fresh)
        attention = (
            (combined[2] / combined[1][..., None])
            .reshape(count_of_rows, QUERY_HEADS * HEAD_SIZE)
            .astype(jnp.bfloat16)
        )
        attention = lax.optimization_barrier(attention).astype(jnp.float32)
        stream = (resid[decode_step_index].astype(jnp.float32) + attention).astype(jnp.bfloat16)
        stream = lax.optimization_barrier(stream).astype(jnp.float32)
        scaled = lax.rsqrt(jnp.mean(stream * stream, axis=-1, keepdims=True) + EPSILON)
        normed = (stream * scaled * gain_scale).astype(jnp.bfloat16)
        own_slice = lax.dynamic_slice_in_dim(normed, seq_index * slice_width, slice_width, 1)
        partial_sums = jnp.dot(
            lax.all_gather(own_slice, "req", axis=0, tiled=True),
            joined,
            preferred_element_type=jnp.float32,
        )
        whole_sums = lax.psum(partial_sums, "seq")
        hidden = (jax.nn.silu(whole_sums[:, :unit_count]) * whole_sums[:, unit_count:]).astype(
            jnp.bfloat16
        )
        down_sum = lax.psum_scatter(
            jnp.dot(hidden, w_down, preferred_element_type=jnp.float32),
            "req",
            scatter_dimension=0,
            tiled=True,
        )
        stream_slice = lax.dynamic_slice_in_dim(stream, seq_index * slice_width, slice_width, 1)
        out_piece = (stream_slice + down_sum).astype(jnp.bfloat16)
        results.append(lax.all_gather(out_piece, "seq", axis=1, tiled=True))
    return jnp.stack(results)


def solution(mesh):
    placed = (
        P(None, "req", None),
        P(None, "req", None),
        P(None, "req", None),
        P("req", "seq", None),
        P("req", "seq", None),
        P("req"),
        P(None, "req", None),
        P(),
        P("seq", "req"),
        P("seq", "req"),
        P("req", "seq"),
    )
    return jax.shard_map(
        body, mesh=mesh, in_specs=placed, out_specs=P(None, "req", None), check_vma=False
    )
```

profile of v0, /device:TPU:24, one launch (start us, length us, event | category | flops | bytes accessed | tf_op | source)
XLA Modules:
  0.0 1327.5 jit_solution(7573360003918362906)
XLA Ops:
  6.5 0.9 fusion.88
  7.5 0.6 copy-done.7
  8.2 1.5 fusion.89
  9.7 0.5 fusion.90
  10.2 0.5 fusion.91
  10.7 0.5 fusion.92
  11.1 260.2 %all-reduce.7 = (f32[8,8,2]{2,1,0:T(8,128)S(1)}, f32[8,8,2]{2,1,0:T(8,128)S(1)}, f32[8,8,2]{2,1,0:T(8,128)S(1)}, f32[8,8,2]{2,1,0:T(8,128)S(1)}) all-reduce(f32[8,8,2]{2,1,0:T(8,128)S(1)} %get-tuple-element.80, f32[8,8,2]{2,1,0:T(8,128)S(1)} %get-tuple-element.78, ...), channel_id=1, replica_groups=mesh['seq'=64,'req'=8] {'seq'}, use_global_device_ids=true, to_apply=%region_29.30 | all-reduce | flops 512 | bytes 4096 | tf_op jit(solution)/shard_map/pmax | solution.py:73
  271.3 0.7 convert_reduce_fusion.5
  272.0 0.9 convolution_multiply_fusion.11
  272.9 0.9 convolution_multiply_fusion.9
  273.8 0.9 convolution_multiply_fusion.7
  274.7 0.9 convolution_multiply_fusion.5
  275.7 0.8 copy-done.1
  276.5 0.3 fusion.94
  276.8 0.3 fusion.93
  277.1 0.2 fusion.59
  277.3 0.2 copy.118
  277.5 0.2 fusion.61
  277.7 0.6 copy-done.5
  278.3 0.3 convert_reduce_fusion.2
  278.6 274.1 %all-reduce.4 = (f32[8,8,2]{2,1,0:T(8,128)S(1)}, f32[8,8,2]{2,1,0:T(8,128)S(1)}, f32[8,8,2]{2,1,0:T(8,128)S(1)}, f32[8,8,2]{2,1,0:T(8,128)S(1)}) all-reduce(f32[8,8,2]{2,1,0:T(8,128)S(1)} %get-tuple-element.88, f32[8,8,2]{2,1,0:T(8,128)S(1)} %get-tuple-element.47, ...), channel_id=1, replica_groups=mesh['seq'=64,'req'=8] {'seq'}, use_global_device_ids=true, to_apply=%region_33.34 | all-reduce | flops 512 | bytes 4096 | tf_op jit(solution)/shard_map/psum | solution.py:75
  552.7 0.3 convert_reduce_fusion
  553.1 0.8 copy-done.6
  554.0 0.1 copy.124
  554.1 0.2 copy.122
  554.3 0.8 dynamic-slice.8
  555.1 1.2 fusion.11
  556.4 0.8 copy-done.13
  557.2 0.4 fusion.12
  557.6 0.8 copy-done.12
  558.4 0.3 fusion.10
  558.7 0.8 copy-done.4
  559.5 0.3 fusion.45
  559.9 0.5 copy-done.3
  560.5 0.1 multiply_reduce_fusion
  560.6 0.1 multiply_reduce_fusion.1
  560.7 0.1 multiply_reduce_fusion.2
  560.9 0.1 multiply_reduce_fusion.3
  561.1 12.0 all_gather.24
  573.1 11.2 all_gather.26
  584.4 0.9 fusion.95
  585.3 0.9 fusion.96
  586.2 11.3 all_gather.28
  597.5 0.9 fusion.97
  598.5 11.2 all_gather.30
  609.7 0.9 fusion.98
  610.7 1.3 dynamic-slice
  612.6 287.1 %all-reduce.12.cloned.1.call-done = (f32[64,1536]{1,0:T(8,128)}, f32[64,1536]{1,0:T(8,128)}, f32[64,1536]{1,0:T(8,128)}, f32[64,1536]{1,0:T(8,128)}) async-done(((f32[64,1536]{1,0:T(8,128)}, f32[64,1536]{1,0:T(8,128)}, f32[64,1536]{1,0:T(8,128)}, f32[64,1536]{1,0:T(8,128)}), (f32[64,1536]{1,0:T(8,128)}, f32[64,1536]{1,0:T(8,128)}, f32[64,1536]{1,0:T(8,128)}, ...) | async-done | bytes 1572880 | tf_op jit(solution)/shard_map/psum | solution.py:101
  899.7 1.2 fusion.33
  901.0 0.2 fusion.35
  901.2 0.8 copy-done.10
  902.0 0.2 fusion.37
  902.2 0.8 copy-done.9
  903.0 0.2 fusion.39
  903.2 24.8 %all-reduce.8 = (f32[64,32]{1,0:T(8,128)S(1)}, f32[64,32]{1,0:T(8,128)S(1)}, f32[64,32]{1,0:T(8,128)S(1)}, f32[64,32]{1,0:T(8,128)S(1)}) all-reduce(f32[64,32]{1,0:T(8,128)S(1)} %fusion.39, f32[64,32]{1,0:T(8,128)S(1)} %fusion.37, f32[64,32]{1,0:T(8,128)S(1)} %fusion.35, ...), channel_id=5, replica_groups=mesh['seq'=64,'req'=8] {'req'}, use_global_device_ids=true, to_apply=%region_37.38.clone | all-reduce | flops 8192 | bytes 65536
  928.0 98.2 %all-gather = bf16[64,32,8]{1,2,0:T(8,128)(2,1)S(1)} all-gather(bf16[1,32,8]{1,2,0:T(8,128)(2,1)S(1)} %fusion.68), channel_id=1, replica_groups=mesh['seq'=64,'req'=8] {'seq'}, dimensions={0}, use_global_device_ids=true | all-gather | bytes 33280 | tf_op jit(solution)/shard_map/all_gather | solution.py:113
  1026.3 0.2 reshape.168
  1026.5 97.5 %all-gather.1 = bf16[64,32,8]{1,2,0:T(8,128)(2,1)S(1)} all-gather(bf16[1,32,8]{1,2,0:T(8,128)(2,1)S(1)} %fusion.69), channel_id=1, replica_groups=mesh['seq'=64,'req'=8] {'seq'}, dimensions={0}, use_global_device_ids=true | all-gather | bytes 33280 | tf_op jit(solution)/shard_map/all_gather | solution.py:113
  1124.1 0.2 reshape.170
  1124.3 97.6 %all-gather.2 = bf16[64,32,8]{1,2,0:T(8,128)(2,1)S(1)} all-gather(bf16[1,32,8]{1,2,0:T(8,128)(2,1)S(1)} %fusion.70), channel_id=1, replica_groups=mesh['seq'=64,'req'=8] {'seq'}, dimensions={0}, use_global_device_ids=true | all-gather | bytes 33280 | tf_op jit(solution)/shard_map/all_gather | solution.py:113
  1222.0 0.2 reshape.172
  1222.2 97.5 %all-gather.3 = bf16[64,32,8]{1,2,0:T(8,128)(2,1)S(1)} all-gather(bf16[1,32,8]{1,2,0:T(8,128)(2,1)S(1)} %fusion.71), channel_id=1, replica_groups=mesh['seq'=64,'req'=8] {'seq'}, dimensions={0}, use_global_device_ids=true | all-gather | bytes 33280 | tf_op jit(solution)/shard_map/all_gather | solution.py:113
  1319.8 0.2 reshape.174
  1320.0 0.7 pad_maximum_fusion
  (75 shorter events, 1.3 us)
Async XLA Ops:
  6.5 265.5 %copy-start = (bf16[8,32,1024]{2,1,0:T(8,128)(2,1)S(1)}, bf16[8,32,1024]{2,1,0:T(8,128)(2,1)}, u32[]{:S(2)}) copy-start(bf16[8,32,1024]{2,1,0:T(8,128)(2,1)} %param.15) | copy-start | bytes 1572868
  6.5 548.6 %all-reduce.14.cloned.1.call-start = ((), (), s32[]{:S(2)}) async-start(), calls=%async_computation.1 | async-start | bytes 524288 | tf_op jit(solution)/shard_map/psum | solution.py:75
  7.4 0.7 copy-start.7
  7.5 2.2 copy-start.8
  275.6 0.8 copy-start.1
  275.6 0.9 copy-start.2
  275.6 624.1 %all-reduce.12.cloned.1.call-start = ((), (), s32[]{:S(2)}) async-start(), calls=%async_computation | async-start | bytes 3145728 | tf_op jit(solution)/shard_map/psum | solution.py:101
  277.5 0.8 copy-start.5
  553.0 0.8 copy-start.6
  556.3 0.8 copy-start.13
  557.5 0.8 copy-start.12
  558.7 0.8 copy-start.4
  559.5 0.9 copy-start.3
  610.6 289.1 %copy-start.14 = (bf16[768,32]{0,1:T(8,128)(2,1)S(1)}, bf16[768,32]{0,1:T(8,128)(2,1)}, u32[]{:S(2)}) copy-start(bf16[768,32]{0,1:T(8,128)(2,1)} %param.21) | copy-start | bytes 147460
  899.7 1.3 copy-start.11
  901.0 1.0 copy-start.10
  902.0 1.0 copy-start.9
Sparse Core Ops, SparseCore 0:
  275.7 275.3 all-reduce.13
  610.8 288.8 all-reduce.11
where the time goes:
time: 1330 us
  blocking collectives  996 us (75%)
  waiting for transfers between devices  287 us (22%)
  matrix products  14.7 us (1%)
  between operations  14.5 us (1%)
    all_gather x4, blocking collectives, body(): results.append(lax.all_gather(out_piece, 'seq', axis=1, tiled=True))  391 us
    psum x1, waiting for transfers between devices, body(): whole_sums = lax.psum(partial_sums, 'seq')  287 us
    psum x1, blocking collectives, body(): lax.psum((factor * local[1], factor[..., None] * local[2]), 'seq')  274 us
    pmax x1, blocking collectives, body(): highest = lax.pmax(local[0], 'seq')  260 us
    all_gather x4, blocking collectives, body(): lax.all_gather(own_slice, 'req', axis=0, tiled=True)  45.8 us
  transfers between devices with their start and end apart: 2, of which 1 were waited for; matrix products, arithmetic and copies ran while one was open for 0% of the time, Pallas kernels for 0%

commit v1 on v0

v1 whole, which is shorter than its diff:
```python
import math

import jax
import jax.numpy as jnp
from jax import lax
from jax.sharding import PartitionSpec as P

QUERY_HEADS = 16
KEY_VALUE_HEADS = 8
HEAD_SIZE = 128
NEG_FILL = -1e30
EPSILON = 1e-06


def partial_softmax(q, keys, values, valid):
    scores = jnp.einsum("rkmd,rbkd->rkmb", q, keys, preferred_element_type=jnp.float32) / math.sqrt(HEAD_SIZE)
    inside = valid[:, None]
    scores = jnp.where(inside, scores, NEG_FILL)
    highest = jnp.max(scores, axis=-1)
    weights = jnp.where(inside, jnp.exp(scores - highest[..., None]), 0.0).astype(jnp.bfloat16)
    totals = jnp.sum(weights.astype(jnp.float32), axis=-1)
    weighted = jnp.einsum("rkmb,rbkd->rkmd", weights, values, preferred_element_type=jnp.float32)
    return highest, totals, weighted


def body(q, nk, nv, kc, vc, cache_len, resid, gain, w_gate, w_up, w_down):
    steps, rows, model = q.shape
    page = kc.shape[1]
    width = w_gate.shape[0]
    units = w_gate.shape[1]
    group = QUERY_HEADS // KEY_VALUE_HEADS
    me = lax.axis_index("seq")
    positions = me * page + jnp.arange(page, dtype=jnp.int32)
    valid = (positions[None, :] < cache_len[:, None])[:, None, :]
    qv = q.reshape(steps, rows, KEY_VALUE_HEADS, group, HEAD_SIZE).transpose(1, 2, 0, 3, 4)
    qv = qv.reshape(rows, KEY_VALUE_HEADS, steps * group, HEAD_SIZE)
    keys = kc.reshape(rows, page, KEY_VALUE_HEADS, HEAD_SIZE)
    values = vc.reshape(rows, page, KEY_VALUE_HEADS, HEAD_SIZE)
    local = partial_softmax(qv, keys, values, jnp.broadcast_to(valid, (rows, steps * group, page)))
    highest = lax.pmax(local[0], "seq")
    factor = jnp.exp(local[0] - highest)
    totals, weighted = lax.psum((factor * local[1], factor[..., None] * local[2]), "seq")
    fk = jnp.swapaxes(nk, 0, 1).reshape(rows, steps, KEY_VALUE_HEADS, HEAD_SIZE)
    fv = jnp.swapaxes(nv, 0, 1).reshape(rows, steps, KEY_VALUE_HEADS, HEAD_SIZE)
    step_of = jnp.arange(steps * group, dtype=jnp.int32) // group
    causal = jnp.arange(steps, dtype=jnp.int32)[None, :] <= step_of[:, None]
    fresh = partial_softmax(qv, fk, fv, jnp.broadcast_to(causal[None], (rows, steps * group, steps)))
    peak = jnp.maximum(highest, fresh[0])
    a = jnp.exp(highest - peak)
    b = jnp.exp(fresh[0] - peak)
    total = a * totals + b * fresh[1]
    acc = a[..., None] * weighted + b[..., None] * fresh[2]
    attn = (acc / total[..., None]).astype(jnp.bfloat16)
    attn = attn.reshape(rows, KEY_VALUE_HEADS, steps, group, HEAD_SIZE).transpose(2, 0, 1, 3, 4)
    attn = attn.reshape(steps, rows, model)
    attn = lax.optimization_barrier(attn).astype(jnp.float32)
    stream = (resid.astype(jnp.float32) + attn).astype(jnp.bfloat16)
    stream = lax.optimization_barrier(stream).astype(jnp.float32)
    scaled = lax.rsqrt(jnp.mean(stream * stream, axis=-1, keepdims=True) + EPSILON)
    normed = (stream * scaled * gain.astype(jnp.float32)).astype(jnp.bfloat16)
    own = lax.dynamic_slice_in_dim(normed, me * width, width, 2)
    every = lax.all_gather(own, "req", axis=1, tiled=True).reshape(-1, width)
    joined = jnp.concatenate([w_gate, w_up], axis=1)
    sums = lax.psum(jnp.dot(every, joined, preferred_element_type=jnp.float32), "seq")
    hidden = (jax.nn.silu(sums[:, :units]) * sums[:, units:]).astype(jnp.bfloat16)
    down = jnp.dot(hidden, w_down, preferred_element_type=jnp.float32)
    down = lax.psum_scatter(down.reshape(steps, -1, width), "req", scatter_dimension=1, tiled=True)
    piece = (lax.dynamic_slice_in_dim(stream, me * width, width, 2) + down).astype(jnp.bfloat16)
    return lax.all_gather(piece, "seq", axis=2, tiled=True)


def solution(mesh):
    placed = (
        P(None, "req", None),
        P(None, "req", None),
        P(None, "req", None),
        P("req", "seq", None),
        P("req", "seq", None),
        P("req"),
        P(None, "req", None),
        P(),
        P("seq", "req"),
        P("seq", "req"),
        P("req", "seq"),
    )
    return jax.shard_map(body, mesh=mesh, in_specs=placed, out_specs=P(None, "req", None), check_vma=False)
```

time: 1330 us -> 989 us (0.74)
  blocking collectives: 996 us -> 673 us
    all_gather x8 -> x2, blocking collectives: 437 us -> 114 us  [the longest x1 100 us: body(): return lax.all_gather(piece, 'seq', axis=2, tiled=True)]
where the time goes in v1:
time: 989 us
  blocking collectives  673 us (68%)
  waiting for transfers between devices  287 us (29%)
  between operations  14.3 us (1%)
    psum x1, waiting for transfers between devices, body(): lax.psum(jnp.dot(every, joined, preferred_element_type=jnp.float32), 'seq')  287 us
    psum x1, blocking collectives, body(): lax.psum((factor * local[1], factor[..., None] * local[2]), 'seq')  274 us
    pmax x1, blocking collectives, body(): highest = lax.pmax(local[0], 'seq')  260 us
    all_gather x1, blocking collectives, body(): return lax.all_gather(piece, 'seq', axis=2, tiled=True)  100 us
    unnamed x1, blocking collectives  24.7 us
  transfers between devices with their start and end apart: 2, of which 1 were waited for; matrix products, arithmetic and copies ran while one was open for 0% of the time, Pallas kernels for 0%

profile of v1, /device:TPU:24, one launch (start us, length us, event | category | flops | bytes accessed | tf_op | source)
XLA Modules:
  0.0 988.6 jit_solution(13132273959055247014)
XLA Ops:
  6.5 0.0 copy-start
  6.5 0.0 all-reduce.4.cloned.1.call-start
  6.5 0.0 copy-start.4
  6.6 1.1 copy.49
  7.6 0.7 broadcast_compare_fusion
  8.4 1.5 fusion.27
  9.8 0.0 copy-start.5
  9.9 260.3 %pmax.7 = f32[8,8,8]{2,1,0:T(8,128)S(1)} all-reduce(f32[8,8,8]{2,1,0:T(8,128)S(1)} %get-tuple-element.10), channel_id=1, replica_groups=mesh['seq'=64,'req'=8] {'seq'}, use_global_device_ids=true, to_apply=%region_1.2 | all-reduce | flops 512 | bytes 4096 | tf_op jit(solution)/shard_map/pmax | solution.py:40
  270.1 0.3 convert_reduce_fusion
  270.4 0.0 copy-done
  270.5 1.0 convolution_multiply_fusion.1
  271.5 0.0 all-reduce.4.cloned.1.call-update
  271.5 0.0 all-reduce.6.cloned.1.call-start
  271.6 0.0 copy-done.4
  271.6 0.0 copy-start.1
  271.6 0.2 fusion.28
  271.8 0.1 convert_reduce_fusion.1
  272.0 0.8 dynamic-slice.2
  272.7 274.0 %psum.22 = f32[8,8,8]{2,1,0:T(8,128)S(1)} all-reduce(f32[8,8,8]{2,1,0:T(8,128)S(1)} %get-tuple-element.8), channel_id=1, replica_groups=mesh['seq'=64,'req'=8] {'seq'}, use_global_device_ids=true, to_apply=%region_5.6 | all-reduce | flops 512 | bytes 4096 | tf_op jit(solution)/shard_map/psum | solution.py:42
  546.8 0.0 all-reduce.4.cloned.1.call-done
  546.8 0.0 copy-done.5
  546.8 0.0 copy-start.2
  546.8 0.0 copy-start.3
  546.9 1.4 fusion.3
  548.2 0.2 copy.54
  548.4 0.0 copy-done.1
  548.5 0.1 multiply_reduce_fusion
  548.6 0.1 multiply_convert_fusion
  548.7 13.1 %all_gather.6 = bf16[4,64,32]{2,0,1:T(4,128)(2,1)S(1)} all-gather(bf16[4,8,32]{2,0,1:T(4,128)(2,1)S(1)} %copy.55), channel_id=1, replica_groups=mesh['seq'=64,'req'=8] {'req'}, dimensions={1}, use_global_device_ids=true | all-gather | bytes 18432 | tf_op jit(solution)/shard_map/all_gather | solution.py:62
  561.7 0.1 copy.56
  561.8 0.1 reshape.71
  562.0 0.0 copy-done.2
  562.0 0.0 copy-done.3
  562.0 0.0 copy-start.6
  562.0 1.5 fusion.12
  563.5 0.0 all-reduce.6.cloned.1.call-update
  563.5 1.3 dynamic-slice
  565.5 286.8 %all-reduce.6.cloned.1.call-done = f32[256,1536]{1,0:T(8,128)} async-done(((f32[256,1536]{1,0:T(8,128)}), f32[256,1536]{1,0:T(8,128)}) %all-reduce.6.cloned.1.call-update) | async-done | bytes 1572880 | tf_op jit(solution)/shard_map/psum | solution.py:64
  852.3 0.0 copy-done.6
  852.3 1.7 fusion.10
  854.0 0.1 reshape.72
  854.1 0.1 copy.57
  854.2 24.7 %all-reduce = f32[4,64,32]{2,0,1:T(4,128)S(1)} all-reduce(f32[4,64,32]{2,0,1:T(4,128)S(1)} %copy.57), channel_id=2, replica_groups=mesh['seq'=64,'req'=8] {'req'}, use_global_device_ids=true, to_apply=%region_9.10.clone | all-reduce | flops 8192 | bytes 65536
  879.0 0.1 fusion.20
  879.0 0.1 copy.59
  879.2 100.5 %all_gather.7 = bf16[4,8,2048]{1,0,2:T(4,128)(2,1)S(1)} all-gather(bf16[4,8,32]{1,0,2:T(4,128)(2,1)S(1)} %copy.59), channel_id=1, replica_groups=mesh['seq'=64,'req'=8] {'seq'}, dimensions={2}, use_global_device_ids=true | all-gather | bytes 133120 | tf_op jit(solution)/shard_map/all_gather | solution.py:69
  979.6 2.1 copy.60
  (10 shorter events, 0.1 us)
Async XLA Ops:
  6.5 263.9 %copy-start = (bf16[8,32,1024]{2,1,0:T(8,128)(2,1)S(1)}, bf16[8,32,1024]{2,1,0:T(8,128)(2,1)}, u32[]{:S(2)}) copy-start(bf16[8,32,1024]{2,1,0:T(8,128)(2,1)} %param.15) | copy-start | bytes 1572868
  6.5 540.3 %all-reduce.4.cloned.1.call-start = ((), (), s32[]{:S(2)}) async-start(), calls=%async_computation | async-start | bytes 524288 | tf_op jit(solution)/shard_map/psum | solution.py:42
  6.5 265.0 %copy-start.4 = (bf16[4,8,1024]{2,1,0:T(8,128)(2,1)S(1)}, bf16[4,8,1024]{2,1,0:T(8,128)(2,1)}, u32[]{:S(2)}) copy-start(bf16[4,8,1024]{2,1,0:T(8,128)(2,1)} %param.12) | copy-start | bytes 196612
  9.8 537.0 %copy-start.5 = (bf16[4,8,1024]{2,1,0:T(8,128)(2,1)S(1)}, bf16[4,8,1024]{2,1,0:T(8,128)(2,1)}, u32[]{:S(2)}) copy-start(bf16[4,8,1024]{2,1,0:T(8,128)(2,1)} %param.13) | copy-start | bytes 196612
  271.5 580.8 %all-reduce.6.cloned.1.call-start = ((), (), s32[]{:S(2)}) async-start(), calls=%async_computation.1 | async-start | bytes 3145728 | tf_op jit(solution)/shard_map/psum | solution.py:64
  271.6 276.8 %copy-start.1 = (bf16[4,8,2048]{2,1,0:T(8,128)(2,1)S(1)}, bf16[4,8,2048]{2,1,0:T(8,128)(2,1)}, u32[]{:S(2)}) copy-start(bf16[4,8,2048]{2,1,0:T(8,128)(2,1)} %param.17) | copy-start | bytes 393220
  546.8 15.1 %copy-start.2 = (bf16[32,768]{1,0:T(8,128)(2,1)S(1)}, bf16[32,768]{1,0:T(8,128)(2,1)}, u32[]{:S(2)}) copy-start(bf16[32,768]{1,0:T(8,128)(2,1)} %param.20) | copy-start | bytes 147460
  546.8 15.1 %copy-start.3 = (bf16[32,768]{1,0:T(8,128)(2,1)S(1)}, bf16[32,768]{1,0:T(8,128)(2,1)}, u32[]{:S(2)}) copy-start(bf16[32,768]{1,0:T(8,128)(2,1)} %param.19) | copy-start | bytes 147460
  562.0 290.3 %copy-start.6 = (bf16[768,32]{0,1:T(8,128)(2,1)S(1)}, bf16[768,32]{0,1:T(8,128)(2,1)}, u32[]{:S(2)}) copy-start(bf16[768,32]{0,1:T(8,128)(2,1)} %param.21) | copy-start | bytes 147460
Sparse Core Ops, SparseCore 0:
  271.6 274.7 all-reduce.3
  563.7 288.5 all-reduce.5

commit v2 on v1

v2 whole, which is shorter than its diff:
```python
import functools
import math

import jax
import jax.numpy as jnp
from jax import lax
from jax.experimental import pallas as pl
from jax.experimental.pallas import tpu as pltpu
from jax.sharding import PartitionSpec as P

NEG_FILL = -1e30
EPSILON = 1e-06
F32 = jnp.float32
BF16 = jnp.bfloat16
NT = (((1,), (1,)), ((), ()))
SCALE = 1.0 / math.sqrt(128)


def split3(x):
    hi = x.astype(BF16).astype(F32)
    rest = x - hi
    mid = rest.astype(BF16).astype(F32)
    low = (rest - mid).astype(BF16).astype(F32)
    return (hi + pltpu.roll(mid, 16, 1) + pltpu.roll(low, 32, 1)).astype(BF16)


def join3(x):
    return x + pltpu.roll(x, 112, 1) + pltpu.roll(x, 96, 1)


def kernel(
    q_h, nk_h, nv_h, k_h, v_h, len_s, resid_h, gain_h, wg_h, wu_h, wd_h,
    out,
    q_v, nk_v, nv_v, k_v, v_v, res_v, gain_v, wg_v, wu_v, wd_v,
    ws, wr, pa, ra, pb, rb, x_v, pp, rp, hh, dd, rd, ee, re,
    lsem,
    ws_s, ws_r, a_s, a_r, b_s, b_r, c_s, c_r, d_s, d_r, e_s, e_r,
    f_s, f_r, g_s, g_r, h_s, h_r, i_s, i_r, j_s, j_r,
):
    s = lax.axis_index("seq")
    q = lax.axis_index("req")
    y = lax.div(s, 16)
    z = lax.rem(s, 16)
    kb = lax.rem(z, 2)
    tg = lax.div(z, 2)
    t = lax.div(z, 4)
    g = lax.rem(tg, 2)
    k = y * 2 + kb
    head = k * 2 + g
    zpair = z + 1 - 2 * kb
    zhi = lax.div(z, 8)
    zlo = lax.rem(z, 8)

    def at(yy, zz):
        return yy * 16 + zz

    y_peers = [(at(lax.rem(y + d, 4), z), q) for d in range(1, 4)]
    z_peers = [(at(y, lax.rem(z + d, 16)), q) for d in range(1, 16)]
    q_peers = [(s, lax.rem(q + d, 8)) for d in range(1, 8)]
    diag_peers = [(at(lax.rem(y + d, 4), zpair), q) for d in range(1, 4)]

    barrier = pltpu.get_barrier_semaphore()
    for peer in y_peers + z_peers + q_peers + diag_peers:
        pl.semaphore_signal(barrier, inc=1, device_id=peer, device_id_type=pl.DeviceIdType.MESH)

    hcol = pl.ds(pl.multiple_of(head * 128, 128), 128)
    kcol = pl.ds(pl.multiple_of(k * 128, 128), 128)
    fcol = pl.ds(pl.multiple_of(k * 256, 256), 256)
    gcol = pl.ds(pl.multiple_of(g * 128, 128), 128)
    loads = [
        (wg_h, wg_v), (wu_h, wu_v), (wd_h, wd_v), (q_h, q_v), (k_h, k_v), (v_h, v_v),
        (nk_h.at[:, :, kcol], nk_v), (nv_h.at[:, :, kcol], nv_v),
        (resid_h.at[t, :, hcol], res_v), (gain_h.at[:, fcol], gain_v),
    ]
    loads = [pltpu.make_async_copy(a, b, lsem.at[i]) for i, (a, b) in enumerate(loads)]
    for c in loads:
        c.start()

    def remote(src, dst, ssem, rsem, peer):
        return pltpu.make_async_remote_copy(
            src_ref=src, dst_ref=dst, send_sem=ssem, recv_sem=rsem,
            device_id=peer, device_id_type=pl.DeviceIdType.MESH,
        )

    sent = []

    def send(copies):
        for c in copies:
            c.start()
        sent.extend(copies)

    for c in loads[:3]:
        c.wait()
    eye = (lax.broadcasted_iota(jnp.int32, (32, 32), 0) == lax.broadcasted_iota(jnp.int32, (32, 32), 1))
    wdt = lax.dot_general(eye.astype(F32).astype(BF16), wd_v[...], NT, preferred_element_type=F32)
    whole = [wg_v[...].astype(F32), wu_v[...].astype(F32), wdt]
    keep = lax.broadcasted_iota(jnp.int32, (32, 128), 1) < 96
    for j in range(8):
        base, off = (96 * j) // 128 * 128, (96 * j) % 128
        for i, w in enumerate(whole):
            if off + 96 <= 128:
                piece = w[:, base:base + 128]
                if off:
                    piece = pltpu.roll(piece, 128 - off, 1)
            else:
                piece = pltpu.roll(w[:, base:base + 256], 256 - off, 1)[:, :128]
            ws[j, :, 128 * i:128 * i + 128] = jnp.where(keep, piece, 0.0).astype(BF16)

    pl.semaphore_wait(barrier, 28)

    for j in range(8):
        zt = 2 * j + zhi
        copy = remote(ws.at[j], wr.at[zlo], ws_s.at[j], ws_r.at[zlo], (at(y, zt), q))

        @pl.when(zt != z)
        def _():
            copy.start()

        @pl.when(zt == z)
        def _():
            wr[zlo] = ws[j]

    for c in loads[3:6]:
        c.wait()
    row = lax.broadcasted_iota(jnp.int32, (64, 256), 0) & 7
    col = lax.broadcasted_iota(jnp.int32, (64, 256), 1)
    limit = jnp.zeros((64, 256), jnp.int32)
    for r in range(8):
        limit = jnp.where(row == r, len_s[r], limit)
    mask = (lax.shift_right_logical(col, 5) == row) & ((col & 31) + s * 32 < limit)
    lane = lax.broadcasted_iota(jnp.int32, (8, 128), 1)
    for yt in range(4):
        tile = jnp.zeros((8, 128), F32)
        for kk in range(2):
            kv = 2 * yt + kk
            qk = jnp.concatenate(
                [
                    q_v[tt, :, 128 * (2 * kv + gg):128 * (2 * kv + gg) + 128].astype(F32)
                    for tt in range(4) for gg in range(2)
                ],
                axis=0,
            ).astype(BF16)
            keys = k_v[:, :, 128 * kv:128 * kv + 128].reshape(256, 128)
            vals = v_v[:, :, 128 * kv:128 * kv + 128].reshape(256, 128)
            sc = lax.dot_general(qk, keys, NT, preferred_element_type=F32) * SCALE
            sc = jnp.where(mask, sc, NEG_FILL)
            top = jnp.max(sc, axis=1, keepdims=True)
            w = jnp.where(mask, jnp.exp(sc - top), 0.0).astype(BF16)
            tot = jnp.sum(w.astype(F32), axis=1, keepdims=True)
            acc = jnp.dot(w, vals, preferred_element_type=F32).astype(BF16)
            pa[yt, 8 * kk:8 * kk + 8] = acc.reshape(8, 8, 128)
            for i in range(8):
                tile = jnp.where(lane == 8 * kk + i, top[8 * i:8 * i + 8], tile)
                tile = jnp.where(lane == 48 + 8 * kk + i, tot[8 * i:8 * i + 8], tile)
        pa[yt, 16] = split3(tile)

    ca = []
    for d in range(1, 4):
        yt = lax.rem(y + d, 4)
        ca.append(remote(pa.at[yt], ra.at[d], a_s.at[d], a_r.at[d], (at(yt, z), q)))
    send(ca)

    for c in loads[6:]:
        c.wait()
    qf = q_v[t, :, hcol]
    nk = nk_v[...].astype(F32).reshape(32, 128).astype(BF16)
    nv = nv_v[...].astype(F32).reshape(32, 128).astype(BF16)
    fs = lax.dot_general(qf, nk, NT, preferred_element_type=F32) * SCALE
    frow = lax.broadcasted_iota(jnp.int32, (8, 32), 0)
    fcl = lax.broadcasted_iota(jnp.int32, (8, 32), 1)
    fmask = ((fcl & 7) == frow) & (lax.shift_right_logical(fcl, 3) <= t)
    fs = jnp.where(fmask, fs, NEG_FILL)
    ftop = jnp.max(fs, axis=1, keepdims=True)
    fw = jnp.where(fmask, jnp.exp(fs - ftop), 0.0).astype(BF16)
    ftot = jnp.sum(fw.astype(F32), axis=1, keepdims=True)
    facc = jnp.dot(fw, nv, preferred_element_type=F32)

    ra[0] = pa[y]
    for c in ca:
        c.wait_recv()
    tiles = [join3(ra[d, 16].astype(F32)) for d in range(4)]
    peak = jnp.maximum(jnp.maximum(tiles[0], tiles[1]), jnp.maximum(tiles[2], tiles[3]))
    fac = [jnp.exp(v - peak) for v in tiles]
    total = sum(pltpu.roll(f, 48, 1) * v for f, v in zip(fac, tiles))
    merged = jnp.where(lane < 16, peak, jnp.where((lane >= 48) & (lane < 64), total, 0.0))
    merged = split3(merged)
    for i in range(16):
        acc = sum(fac[d][:, i:i + 1] * ra[d, i].astype(F32) for d in range(4))
        zt = 2 * (i % 8) + i // 8
        pb[zt, 0] = acc.astype(BF16)
        pb[zt, 1] = merged

    cb = []
    for d in range(1, 16):
        zt = lax.rem(z + d, 16)
        cb.append(remote(pb.at[zt], rb.at[d], b_s.at[d], b_r.at[d], (at(y, zt), q)))
    send(cb)
    rb[0] = pb[z]
    for c in cb:
        c.wait_recv()
    own = kb * 8 + tg
    lane3 = lax.broadcasted_iota(jnp.int32, (16, 8, 128), 2)
    mine = (lane3 & 15) == own
    ml = rb[:, 1].astype(F32)
    m = jnp.sum(jnp.where(mine & (lane3 < 48), ml, 0.0), axis=2, keepdims=True)
    l = jnp.sum(jnp.where(mine & (lane3 >= 48), ml, 0.0), axis=2, keepdims=True)
    peak = jnp.maximum(jnp.max(m, axis=0), ftop)
    f = jnp.exp(m - peak[None])
    ff = jnp.exp(ftop - peak)
    total = jnp.sum(f * l, axis=0) + ff * ftot
    acc = jnp.sum(f * rb[:, 0].astype(F32), axis=0) + ff * facc
    attn = (acc / total).astype(BF16).astype(F32)
    stream = (res_v[...].astype(F32) + attn).astype(BF16)
    x_v[q, t, :, gcol] = stream

    cc = []
    for d in range(1, 8):
        zt = lax.rem(z + 2 * d, 16)
        ref = x_v.at[q, t, :, gcol]
        cc.append(remote(ref, ref, c_s.at[d], c_r.at[d], (at(y, zt), q)))
    send(cc)
    for c in cc:
        c.wait_recv()
    cd = []
    for d in range(1, 8):
        ref = x_v.at[q]
        cd.append(remote(ref, ref, d_s.at[d], d_r.at[d], (s, lax.rem(q + d, 8))))
    send(cd)
    for f8 in range(8):
        copy = remote(ws.at[f8], wr.at[f8], ws_s.at[f8], ws_r.at[f8], (s, q))

        @pl.when(8 * kb + f8 != z)
        def _():
            copy.wait_recv()
    for c in cd:
        c.wait_recv()

    xf = x_v[...].astype(F32).reshape(256, 256)
    square = jnp.sum(xf * xf, axis=1, keepdims=True)
    xg = (xf * gain_v[...].astype(F32)).astype(BF16)
    gu = jnp.dot(xg, wr[:, :, 0:256].reshape(256, 256), preferred_element_type=F32)
    hi = square.astype(BF16).astype(F32)
    lane2 = lax.broadcasted_iota(jnp.int32, (256, 256), 1)
    gu = jnp.where(lane2 == 96, hi, jnp.where(lane2 == 97, square - hi, gu))
    pp[...] = gu.astype(BF16).reshape(8, 32, 256)
    k_targets = []
    for dy in range(4):
        for dk in range(2):
            if dy or dk:
                yt = lax.rem(y + dy, 4)
                zt = zpair if dk else z
                kt = yt * 2 + (1 - kb if dk else kb)
                k_targets.append((2 * dy + dk, kt, (at(yt, zt), q)))
    ce = [remote(pp.at[kt], rp.at[d], e_s.at[d], e_r.at[d], peer) for d, kt, peer in k_targets]
    send(ce)
    rp[0] = pp[k]
    for c in ce:
        c.wait_recv()
    gu = jnp.sum(rp[...].astype(F32), axis=0)
    lane32 = lax.broadcasted_iota(jnp.int32, (32, 128), 1)
    gate, up = gu[:, :128], gu[:, 128:]
    square = jnp.sum(jnp.where((lane32 == 96) | (lane32 == 97), gate, 0.0), axis=1, keepdims=True)
    norm = lax.rsqrt(square * (1.0 / 2048) + EPSILON)
    gate = gate * norm
    up = up * norm
    hidden = gate / (1.0 + jnp.exp(-gate)) * up
    hh[k] = jnp.where(lane32 < 96, hidden, 0.0).astype(BF16)
    cf = []
    for d, kt, peer in k_targets:
        cf.append(remote(hh.at[k], hh.at[k], f_s.at[d], f_r.at[d], peer))
    send(cf)
    for c in cf:
        c.wait_recv()

    down = lax.dot_general(
        hh[...].reshape(256, 128), wr[:, :, 256:384].reshape(256, 128), NT, preferred_element_type=F32
    )
    dd[...] = down.astype(BF16).reshape(8, 32, 256)
    cg = []
    for d in range(1, 8):
        qt = lax.rem(q + d, 8)
        cg.append(remote(dd.at[qt], rd.at[d], g_s.at[d], g_r.at[d], (s, qt)))
    send(cg)
    rd[0] = dd[q]
    for c in cg:
        c.wait_recv()
    down = jnp.sum(rd[...].astype(F32), axis=0)
    for i in range(8):
        tt, gg = i // 2, i % 2
        ee[i] = down[8 * tt:8 * tt + 8, 128 * gg:128 * gg + 128].astype(BF16)
    ch = []
    for d in range(1, 8):
        zt = lax.rem(z + 2 * d, 16)
        ch.append(remote(ee.at[lax.div(zt, 2)], re.at[d], h_s.at[d], h_r.at[d], (at(y, zt), q)))
    send(ch)
    re[0] = ee[tg]
    for c in ch:
        c.wait_recv()
    final = stream.astype(F32) + jnp.sum(re[...].astype(F32), axis=0)
    out[t, :, hcol] = final.astype(BF16)

    ci = []
    for d in range(1, 16):
        ref = out.at[t, :, hcol]
        ci.append(remote(ref, ref, i_s.at[d], i_r.at[d], (at(y, lax.rem(z + d, 16)), q)))
    send(ci)
    for c in ci:
        c.wait_recv()
    cj = []
    for d in range(1, 4):
        ref = out.at[:, :, pl.ds(pl.multiple_of(y * 512, 512), 512)]
        cj.append(remote(ref, ref, j_s.at[d], j_r.at[d], (at(lax.rem(y + d, 4), z), q)))
    send(cj)
    for c in cj:
        c.wait_recv()

    for c in sent:
        c.wait_send()
    for j in range(8):
        zt = 2 * j + zhi
        copy = remote(ws.at[j], wr.at[zlo], ws_s.at[j], ws_r.at[zlo], (at(y, zt), q))

        @pl.when(zt != z)
        def _():
            copy.wait_send()


def step(q, nk, nv, kc, vc, cache_len, resid, gain, w_gate, w_up, w_down):
    hbm = pl.BlockSpec(memory_space=pl.ANY)
    dma = lambda n: pltpu.SemaphoreType.DMA((n,))
    vm = pltpu.VMEM
    sems = []
    for n in (8, 4, 16, 8, 8, 8, 8, 8, 8, 16, 4):
        sems += [dma(n), dma(n)]
    return pl.pallas_call(
        kernel,
        out_shape=jax.ShapeDtypeStruct((4, 8, 2048), BF16),
        in_specs=[hbm] * 5 + [pl.BlockSpec(memory_space=pltpu.SMEM)] + [hbm] * 5,
        out_specs=pl.BlockSpec(memory_space=pltpu.VMEM),
        scratch_shapes=[
            vm((4, 8, 2048), BF16), vm((4, 8, 128), BF16), vm((4, 8, 128), BF16),
            vm((8, 32, 1024), BF16), vm((8, 32, 1024), BF16), vm((8, 128), BF16), vm((1, 256), BF16),
            vm((32, 768), BF16), vm((32, 768), BF16), vm((768, 32), BF16),
            vm((8, 32, 384), BF16), vm((8, 32, 384), BF16),
            vm((4, 17, 8, 128), BF16), vm((4, 17, 8, 128), BF16),
            vm((16, 2, 8, 128), BF16), vm((16, 2, 8, 128), BF16),
            vm((8, 4, 8, 256), BF16),
            vm((8, 32, 256), BF16), vm((8, 32, 256), BF16),
            vm((8, 32, 128), BF16),
            vm((8, 32, 256), BF16), vm((8, 32, 256), BF16),
            vm((8, 8, 128), BF16), vm((8, 8, 128), BF16),
            dma(10),
        ] + sems,
        compiler_params=pltpu.CompilerParams(
            collective_id=0, has_side_effects=True, vmem_limit_bytes=16 * 1024 * 1024
        ),
    )(q, nk, nv, kc, vc, cache_len, resid, gain.reshape(1, 2048), w_gate, w_up, w_down)


def solution(mesh):
    placed = (
        P(None, "req", None),
        P(None, "req", None),
        P(None, "req", None),
        P("req", "seq", None),
        P("req", "seq", None),
        P("req"),
        P(None, "req", None),
        P(),
        P("seq", "req"),
        P("seq", "req"),
        P("req", "seq"),
    )
    return jax.shard_map(step, mesh=mesh, in_specs=placed, out_specs=P(None, "req", None), check_vma=False)
```

time: 989 us -> 85.2 us (0.09)
  the two profiles are of different devices: /device:TPU:24 before, /device:TPU:4 now
where the time goes in v2:
time: 85.2 us; the launch traced here: 84.9 us
  Pallas kernels  77.8 us (91%)
  local copies, waits for them, and re-layouts  7.03 us (8%)
    pallas_call x1, Pallas kernels, step(): pl.pallas_call(kernel, out_shape=jax.ShapeDtypeStruct((4, 8, 2048), BF16)...  77.8 us
    unnamed x20, local copies, waits for them, and re-layouts  6.3 us

profile of v2, /device:TPU:4, one launch (start us, length us, event | category | flops | bytes accessed | tf_op | source)
XLA Modules:
  0.0 84.9 jit_solution(12598874936066039744)
XLA Ops:
  0.0 0.0 copy-start.2
  0.0 0.7 reshape.3.gain_h
  0.7 0.0 copy-start.4
  0.7 0.0 copy-start.6
  0.7 0.0 copy-start.8
  0.8 1.0 %copy.12.wd_h = bf16[768,32]{1,0:T(8,128)(2,1)S(1)} copy(bf16[768,32]{0,1:T(8,128)(2,1)} %param.21) | data formatting | bytes 98304 | tf_op args[10]
  1.8 0.0 copy-done.2
  1.8 0.0 copy-done.4
  1.8 0.0 copy-done.6
  1.8 0.0 copy-done.8
  1.8 0.0 copy-start
  1.8 1.0 %copy-done = bf16[8,32,1024]{2,1,0:T(8,128)(2,1)S(1)} copy-done((bf16[8,32,1024]{2,1,0:T(8,128)(2,1)S(1)}, bf16[8,32,1024]{2,1,0:T(8,128)(2,1)}, u32[]{:S(2)}) %copy-start) | copy-done | bytes 524312
  2.8 0.0 copy-start.1
  2.9 1.0 %copy-done.1 = bf16[8,32,1024]{2,1,0:T(8,128)(2,1)S(1)} copy-done((bf16[8,32,1024]{2,1,0:T(8,128)(2,1)S(1)}, bf16[8,32,1024]{2,1,0:T(8,128)(2,1)}, u32[]{:S(2)}) %copy-start.1) | copy-done | bytes 524312
  3.9 0.0 copy-start.3
  3.9 0.9 %copy-done.3 = bf16[4,8,2048]{2,1,0:T(8,128)(2,1)S(1)} copy-done((bf16[4,8,2048]{2,1,0:T(8,128)(2,1)S(1)}, bf16[4,8,2048]{2,1,0:T(8,128)(2,1)}, u32[]{:S(2)}) %copy-start.3) | copy-done | bytes 131096
  4.8 0.0 copy-start.5
  4.8 0.8 copy-done.5
  5.6 0.0 copy-start.7
  5.6 0.8 copy-done.7
  6.4 77.8 %shard_map.109 = bf16[4,8,2048]{2,1,0:T(8,128)(2,1)S(1)} custom-call(bf16[4,8,2048]{2,1,0:T(8,128)(2,1)S(1)} %copy-done.2, bf16[4,8,1024]{2,1,0:T(8,128)(2,1)S(1)} %copy-done.4, bf16[4,8,1024]{2,1,0:T(8,128)(2,1)S(1)} %copy-done.5, bf16[8,32,1024]{2,1,0:T(8,128)(2,1)S(1)} %copy-done, bf16[8,32,1024]{2,1,0:T(8,128)(2,1)S(1)} %copy-done.1, s32[8]{0:T(128)S(1)} %copy-done.8, ...), custom_call_target="tpu_custom_call" | custom-call | tf_op jit(solution)/shard_map/pallas_call | solution.py:335
  84.2 0.7 copy.14
Async XLA Ops:
  0.0 1.8 %copy-start.2 = (bf16[4,8,2048]{2,1,0:T(8,128)(2,1)S(1)}, bf16[4,8,2048]{2,1,0:T(8,128)(2,1)}, u32[]{:S(2)}) copy-start(bf16[4,8,2048]{2,1,0:T(8,128)(2,1)} %q_h.1) | copy-start | bytes 393220
  0.7 1.0 %copy-start.4 = (bf16[4,8,1024]{2,1,0:T(8,128)(2,1)S(1)}, bf16[4,8,1024]{2,1,0:T(8,128)(2,1)}, u32[]{:S(2)}) copy-start(bf16[4,8,1024]{2,1,0:T(8,128)(2,1)} %nk_h.1) | copy-start | bytes 196612
  0.7 1.1 %copy-start.6 = (bf16[32,768]{1,0:T(8,128)(2,1)S(1)}, bf16[32,768]{1,0:T(8,128)(2,1)}, u32[]{:S(2)}) copy-start(bf16[32,768]{1,0:T(8,128)(2,1)} %wg_h.1) | copy-start | bytes 147460
  0.7 1.1 %copy-start.8 = (s32[8]{0:T(128)S(1)}, s32[8]{0:T(128)}, u32[]{:S(2)}) copy-start(s32[8]{0:T(128)} %len_s.1) | copy-start | bytes 100
  1.8 1.0 %copy-start = (bf16[8,32,1024]{2,1,0:T(8,128)(2,1)S(1)}, bf16[8,32,1024]{2,1,0:T(8,128)(2,1)}, u32[]{:S(2)}) copy-start(bf16[8,32,1024]{2,1,0:T(8,128)(2,1)} %k_h.1) | copy-start | bytes 1572868
  2.8 1.0 %copy-start.1 = (bf16[8,32,1024]{2,1,0:T(8,128)(2,1)S(1)}, bf16[8,32,1024]{2,1,0:T(8,128)(2,1)}, u32[]{:S(2)}) copy-start(bf16[8,32,1024]{2,1,0:T(8,128)(2,1)} %v_h.1) | copy-start | bytes 1572868
  3.9 0.9 %copy-start.3 = (bf16[4,8,2048]{2,1,0:T(8,128)(2,1)S(1)}, bf16[4,8,2048]{2,1,0:T(8,128)(2,1)}, u32[]{:S(2)}) copy-start(bf16[4,8,2048]{2,1,0:T(8,128)(2,1)} %resid_h.1) | copy-start | bytes 393220
  4.8 0.8 copy-start.5
  5.6 0.8 copy-start.7

commit v3 on v2

v3 whole, which is shorter than its diff:
```python
import functools
import math

import jax
import jax.numpy as jnp
from jax import lax
from jax.experimental import pallas as pl
from jax.experimental.pallas import tpu as pltpu
from jax.sharding import PartitionSpec as P

NEG_FILL = -1e30
EPSILON = 1e-06
F32 = jnp.float32
BF16 = jnp.bfloat16
NT = (((1,), (1,)), ((), ()))
SCALE = 1.0 / math.sqrt(128)


def split3(x):
    hi = x.astype(BF16).astype(F32)
    rest = x - hi
    mid = rest.astype(BF16).astype(F32)
    low = (rest - mid).astype(BF16).astype(F32)
    return (hi + pltpu.roll(mid, 16, 1) + pltpu.roll(low, 32, 1)).astype(BF16)


def join3(x):
    return x + pltpu.roll(x, 112, 1) + pltpu.roll(x, 96, 1)


def kernel(
    q_h, nk_h, nv_h, k_h, v_h, len_s, resid_h, gain_h, wg_h, wu_h, wd_h,
    out,
    q_v, nk_v, nv_v, k_v, v_v, res_v, gain_v, wg_v, wu_v, wd_v,
    ws, wr, pa, ra, pb, rb, x_v, pp, rp, hh, dd, rd, ee, re,
    lsem,
    ws_s, ws_r, a_s, a_r, b_s, b_r, c_s, c_r, d_s, d_r, e_s, e_r, f_s, f_r, g_s, g_r, h_s, h_r,
):
    s = lax.axis_index("seq")
    q = lax.axis_index("req")
    y = lax.div(s, 16)
    z = lax.rem(s, 16)
    kb = lax.rem(z, 2)
    tg = lax.div(z, 2)
    k = y * 2 + kb
    zpair = z + 1 - 2 * kb
    zhi = lax.div(z, 8)
    zlo = lax.rem(z, 8)

    def at(yy, zz):
        return yy * 16 + zz

    k_peers = []
    for dy in range(4):
        for dk in range(2):
            if dy or dk:
                yt = lax.rem(y + dy, 4)
                kt = yt * 2 + (1 - kb if dk else kb)
                k_peers.append((2 * dy + dk, kt, (at(yt, zpair if dk else z), q)))
    t_peers = []
    for d in range(1, 8):
        zt = lax.rem(z + 2 * d, 16)
        t_peers.append((d, lax.div(zt, 2), (at(y, zt), q)))
    q_peers = [(d, lax.rem(q + d, 8), (s, lax.rem(q + d, 8))) for d in range(1, 8)]
    odd_z = [(at(y, lax.rem(zpair + 2 * d, 16)), q) for d in range(1, 8)]

    barrier = pltpu.get_barrier_semaphore()
    for peer in [p[2] for p in k_peers + t_peers + q_peers] + odd_z:
        pl.semaphore_signal(barrier, inc=1, device_id=peer, device_id_type=pl.DeviceIdType.MESH)

    kcol = pl.ds(pl.multiple_of(k * 128, 128), 128)
    fcol = pl.ds(pl.multiple_of(k * 256, 256), 256)
    loads = [
        (wg_h, wg_v), (wu_h, wu_v), (wd_h, wd_v), (q_h, q_v), (k_h, k_v), (v_h, v_v),
        (nk_h.at[:, :, kcol], nk_v), (nv_h.at[:, :, kcol], nv_v),
        (resid_h.at[:, :, fcol], res_v), (gain_h, gain_v),
    ]
    loads = [pltpu.make_async_copy(a, b, lsem.at[i]) for i, (a, b) in enumerate(loads)]
    for c in loads:
        c.start()

    def remote(src, dst, ssem, rsem, peer):
        return pltpu.make_async_remote_copy(
            src_ref=src, dst_ref=dst, send_sem=ssem, recv_sem=rsem,
            device_id=peer, device_id_type=pl.DeviceIdType.MESH,
        )

    sent = []

    def send(copies):
        for c in copies:
            c.start()
        sent.extend(copies)
        return copies

    for c in loads[:3]:
        c.wait()
    whole = [wg_v[...].astype(F32), wu_v[...].astype(F32), wd_v[...].astype(F32)]
    keep = lax.broadcasted_iota(jnp.int32, (32, 128), 1) < 96
    for j in range(8):
        base, off = (96 * j) // 128 * 128, (96 * j) % 128
        for i, w in enumerate(whole):
            if off + 96 <= 128:
                piece = w[:, base:base + 128]
                if off:
                    piece = pltpu.roll(piece, 128 - off, 1)
            else:
                piece = pltpu.roll(w[:, base:base + 256], 256 - off, 1)[:, :128]
            ws[j, :, 128 * i:128 * i + 128] = jnp.where(keep, piece, 0.0).astype(BF16)

    for c in loads[3:6]:
        c.wait()
    row = lax.broadcasted_iota(jnp.int32, (64, 256), 0) & 7
    col = lax.broadcasted_iota(jnp.int32, (64, 256), 1)
    limit = jnp.zeros((64, 256), jnp.int32)
    for r in range(8):
        limit = jnp.where(row == r, len_s[r], limit)
    mask = (lax.shift_right_logical(col, 5) == row) & ((col & 31) + s * 32 < limit)
    lane = lax.broadcasted_iota(jnp.int32, (8, 128), 1)

    def stats(top, tot):
        tile = jnp.zeros((8, 128), F32)
        for i in range(8):
            tile = jnp.where(lane == i, top[8 * i:8 * i + 8], tile)
            tile = jnp.where(lane == 48 + i, tot[8 * i:8 * i + 8], tile)
        return tile

    for kv in range(8):
        qk = jnp.concatenate(
            [
                q_v[tt, :, 128 * (2 * kv + gg):128 * (2 * kv + gg) + 128].astype(F32)
                for tt in range(4) for gg in range(2)
            ],
            axis=0,
        ).astype(BF16)
        keys = k_v[:, :, 128 * kv:128 * kv + 128].reshape(256, 128)
        vals = v_v[:, :, 128 * kv:128 * kv + 128].reshape(256, 128)
        sc = lax.dot_general(qk, keys, NT, preferred_element_type=F32) * SCALE
        sc = jnp.where(mask, sc, NEG_FILL)
        top = jnp.max(sc, axis=1, keepdims=True)
        w = jnp.where(mask, jnp.exp(sc - top), 0.0).astype(BF16)
        tot = jnp.sum(w.astype(F32), axis=1, keepdims=True)
        acc = jnp.dot(w, vals, preferred_element_type=F32).astype(BF16)
        pa[kv, 0:8] = acc.reshape(8, 8, 128)
        pa[kv, 8] = split3(stats(top, tot))

    pl.semaphore_wait(barrier, 28)

    ca = send([remote(pa.at[kt], ra.at[d], a_s.at[d], a_r.at[d], peer) for d, kt, peer in k_peers])

    for j in range(8):
        zt = 2 * j + zhi
        copy = remote(ws.at[j], wr.at[zlo], ws_s.at[j], ws_r.at[zlo], (at(y, zt), q))

        @pl.when(zt != z)
        def _():
            copy.start()

        @pl.when(zt == z)
        def _():
            wr[zlo] = ws[j]

    for c in loads[6:]:
        c.wait()
    qf = jnp.concatenate(
        [
            q_v[tt, :, pl.ds(pl.multiple_of(k * 256 + 128 * gg, 128), 128)].astype(F32)
            for tt in range(4) for gg in range(2)
        ],
        axis=0,
    ).astype(BF16)
    nk = nk_v[...].astype(F32).reshape(32, 128).astype(BF16)
    nv = nv_v[...].astype(F32).reshape(32, 128).astype(BF16)
    fs = lax.dot_general(qf, nk, NT, preferred_element_type=F32) * SCALE
    frow = lax.broadcasted_iota(jnp.int32, (64, 32), 0)
    fcl = lax.broadcasted_iota(jnp.int32, (64, 32), 1)
    fmask = ((fcl & 7) == (frow & 7)) & (lax.shift_right_logical(fcl, 3) <= lax.shift_right_logical(frow, 4))
    fs = jnp.where(fmask, fs, NEG_FILL)
    ftop = jnp.max(fs, axis=1, keepdims=True)
    fw = jnp.where(fmask, jnp.exp(fs - ftop), 0.0).astype(BF16)
    ftot = jnp.sum(fw.astype(F32), axis=1, keepdims=True)
    facc = jnp.dot(fw, nv, preferred_element_type=F32)
    fstat = stats(ftop, ftot)

    def merge(parts):
        peak = functools.reduce(jnp.maximum, parts)
        fac = [jnp.exp(v - peak) for v in parts]
        total = sum(pltpu.roll(f, 48, 1) * v for f, v in zip(fac, parts))
        return peak, fac, total

    ra[0] = pa[k]
    for c in ca:
        c.wait_recv()
    peak, fac, total = merge([join3(ra[d, 8].astype(F32)) for d in range(8)])
    for i in range(8):
        pb[i] = sum(fac[d][:, i:i + 1] * ra[d, i].astype(F32) for d in range(8)).astype(BF16)
    pb[8] = split3(jnp.where(lane < 8, peak, jnp.where((lane >= 48) & (lane < 56), total, 0.0)))

    cb = send([remote(pb, rb.at[tg], b_s.at[d], b_r.at[d], peer) for d, _, peer in t_peers])
    rb[tg] = pb[...]
    for c in cb:
        c.wait_recv()
    _, fac, total = merge([join3(rb[d, 8].astype(F32)) for d in range(8)] + [fstat])
    inverse = pltpu.roll(total, 80, 1)
    for i in range(8):
        acc = sum(fac[d][:, i:i + 1] * rb[d, i].astype(F32) for d in range(8))
        acc = acc + fac[8][:, i:i + 1] * facc[8 * i:8 * i + 8]
        attn = (acc / inverse[:, i:i + 1]).astype(BF16).astype(F32)
        tt, gg = i // 2, i % 2
        x_v[q, tt, :, 128 * gg:128 * gg + 128] = (
            res_v[tt, :, 128 * gg:128 * gg + 128].astype(F32) + attn
        ).astype(BF16)

    cd = send([remote(x_v.at[q], x_v.at[q], d_s.at[d], d_r.at[d], peer) for d, _, peer in q_peers])
    for f8 in range(8):
        copy = remote(ws.at[f8], wr.at[f8], ws_s.at[f8], ws_r.at[f8], (s, q))

        @pl.when(8 * kb + f8 != z)
        def _():
            copy.wait_recv()
    for c in cd:
        c.wait_recv()

    xf = x_v[...].astype(F32).reshape(256, 256)
    square = jnp.sum(xf * xf, axis=1, keepdims=True)
    xg = (xf * gain_v[fcol].astype(F32).reshape(1, 256)).astype(BF16)
    gu = jnp.dot(xg, wr[:, :, 0:256].reshape(256, 256), preferred_element_type=F32)
    hi = square.astype(BF16).astype(F32)
    lane2 = lax.broadcasted_iota(jnp.int32, (256, 256), 1)
    gu = jnp.where(lane2 == 96, hi, jnp.where(lane2 == 97, square - hi, gu))
    pp[...] = gu.astype(BF16).reshape(8, 32, 256)
    ce = send([remote(pp.at[kt], rp.at[d], e_s.at[d], e_r.at[d], peer) for d, kt, peer in k_peers])
    rp[0] = pp[k]
    for c in ce:
        c.wait_recv()
    gu = jnp.sum(rp[...].astype(F32), axis=0)
    lane32 = lax.broadcasted_iota(jnp.int32, (32, 128), 1)
    gate, up = gu[:, :128], gu[:, 128:]
    square = jnp.sum(jnp.where((lane32 == 96) | (lane32 == 97), gate, 0.0), axis=1, keepdims=True)
    norm = lax.rsqrt(square * (1.0 / 2048) + EPSILON)
    gate = gate * norm
    up = up * norm
    hidden = gate / (1.0 + jnp.exp(-gate)) * up
    hh[k] = jnp.where(lane32 < 96, hidden, 0.0).astype(BF16)
    cf = send([remote(hh.at[k], hh.at[k], f_s.at[d], f_r.at[d], peer) for d, _, peer in k_peers])
    for c in cf:
        c.wait_recv()

    down = lax.dot_general(
        hh[...].reshape(256, 128), wr[:, :, 256:384].reshape(256, 128), NT, preferred_element_type=F32
    )
    dd[...] = down.astype(BF16).reshape(8, 32, 256)
    cg = send([remote(dd.at[qt], rd.at[d], g_s.at[d], g_r.at[d], peer) for d, qt, peer in q_peers])
    rd[0] = dd[q]
    for c in cg:
        c.wait_recv()
    ee[...] = jnp.sum(rd[...].astype(F32), axis=0).astype(BF16)
    ch = send([remote(ee, re.at[tg], h_s.at[d], h_r.at[d], peer) for d, _, peer in t_peers])
    re[tg] = ee[...]
    for c in ch:
        c.wait_recv()
    final = x_v[q].astype(F32) + jnp.sum(re[...].astype(F32), axis=0).reshape(4, 8, 256)
    out[:, :, fcol] = final.astype(BF16)

    ci = send([remote(out.at[:, :, fcol], out.at[:, :, fcol], c_s.at[d], c_r.at[d], peer) for d, _, peer in k_peers])
    for c in ci:
        c.wait_recv()

    for c in sent:
        c.wait_send()
    for j in range(8):
        zt = 2 * j + zhi
        copy = remote(ws.at[j], wr.at[zlo], ws_s.at[j], ws_r.at[zlo], (at(y, zt), q))

        @pl.when(zt != z)
        def _():
            copy.wait_send()


def step(q, nk, nv, kc, vc, cache_len, resid, gain, w_gate, w_up, w_down):
    hbm = pl.BlockSpec(memory_space=pl.ANY)
    dma = lambda n: pltpu.SemaphoreType.DMA((n,))
    vm = pltpu.VMEM
    sems = []
    for _ in range(9):
        sems += [dma(8), dma(8)]
    return pl.pallas_call(
        kernel,
        out_shape=jax.ShapeDtypeStruct((4, 8, 2048), BF16),
        in_specs=[hbm] * 5 + [pl.BlockSpec(memory_space=pltpu.SMEM)] + [hbm] * 5,
        out_specs=pl.BlockSpec(memory_space=pltpu.VMEM),
        scratch_shapes=[
            vm((4, 8, 2048), BF16), vm((4, 8, 128), BF16), vm((4, 8, 128), BF16),
            vm((8, 32, 1024), BF16), vm((8, 32, 1024), BF16), vm((4, 8, 256), BF16), vm((2048,), BF16),
            vm((32, 768), BF16), vm((32, 768), BF16), vm((32, 768), BF16),
            vm((8, 32, 384), BF16), vm((8, 32, 384), BF16),
            vm((8, 9, 8, 128), BF16), vm((8, 9, 8, 128), BF16),
            vm((9, 8, 128), BF16), vm((8, 9, 8, 128), BF16),
            vm((8, 4, 8, 256), BF16),
            vm((8, 32, 256), BF16), vm((8, 32, 256), BF16),
            vm((8, 32, 128), BF16),
            vm((8, 32, 256), BF16), vm((8, 32, 256), BF16),
            vm((32, 256), BF16), vm((8, 32, 256), BF16),
            dma(10),
        ] + sems,
        compiler_params=pltpu.CompilerParams(
            collective_id=0, has_side_effects=True, vmem_limit_bytes=60 * 1024 * 1024
        ),
    )(q, nk, nv, kc, vc, cache_len, resid, gain, w_gate, w_up, w_down.T)


def solution(mesh):
    placed = (
        P(None, "req", None),
        P(None, "req", None),
        P(None, "req", None),
        P("req", "seq", None),
        P("req", "seq", None),
        P("req"),
        P(None, "req", None),
        P(),
        P("seq", "req"),
        P("seq", "req"),
        P("req", "seq"),
    )
    return jax.shard_map(step, mesh=mesh, in_specs=placed, out_specs=P(None, "req", None), check_vma=False)
```

time: 85.2 us -> 74.7 us (0.88)
  the two profiles are of different devices: /device:TPU:4 before, /device:TPU:24 now
where the time goes in v3:
time: 74.7 us; the launch traced here: 73.7 us
  Pallas kernels  72.1 us (97%)
  local copies, waits for them, and re-layouts  1.57 us (2%)
    pallas_call x1, Pallas kernels, step(): pl.pallas_call(kernel, out_shape=jax.ShapeDtypeStruct((4, 8, 2048), BF16)...  72.1 us
    unnamed x1, local copies, waits for them, and re-layouts  1.57 us

profile of v3, /device:TPU:24, one launch (start us, length us, event | category | flops | bytes accessed | tf_op | source)
XLA Modules:
  0.0 73.7 jit_solution(7232170510933550060)
XLA Ops:
  0.0 72.1 %shard_map.109 = bf16[4,8,2048]{2,1,0:T(8,128)(2,1)} custom-call(bf16[4,8,2048]{2,1,0:T(8,128)(2,1)} %q_h.1, bf16[4,8,1024]{2,1,0:T(8,128)(2,1)} %nk_h.1, bf16[4,8,1024]{2,1,0:T(8,128)(2,1)} %nv_h.1, bf16[8,32,1024]{2,1,0:T(8,128)(2,1)} %k_h.1, bf16[8,32,1024]{2,1,0:T(8,128)(2,1)} %v_h.1, s32[8]{0:T(128)} %len_s.1, bf16[4,8,2048]{2,1,0:T(8,128)(2,1)} %resid_h.1, ...), custom_call_target="tpu_custom_call" | custom-call | tf_op jit(solution)/shard_map/pallas_call | solution.py:287
  72.1 1.6 %copy.13 = bf16[4,8,2048]{2,1,0:T(8,128)(2,1)} copy(bf16[4,8,2048]{2,1,0:T(8,128)(2,1)} %shard_map.109) | data formatting | bytes 262144

commit v4 on v3

--- a/solution.py
+++ b/solution.py
@@ -41,15 +41,32 @@
     y = lax.div(s, 16)
     z = lax.rem(s, 16)
     kb = lax.rem(z, 2)
-    tg = lax.div(z, 2)
     k = y * 2 + kb
     zpair = z + 1 - 2 * kb
+    zh = lax.div(z, 4)
+    zl = lax.rem(z, 4)
+    half = lax.div(zl, 2)
     zhi = lax.div(z, 8)
     zlo = lax.rem(z, 8)
 
     def at(yy, zz):
         return yy * 16 + zz
 
+    a_peers = []
+    for dy in range(4):
+        for dz in range(4):
+            if dy or dz:
+                yt, zt = lax.rem(y + dy, 4), lax.rem(zl + dz, 4)
+                kt, ht = yt * 2 + lax.rem(zt, 2), lax.div(zt, 2)
+                a_peers.append((4 * dy + dz, kt, ht, (at(yt, 4 * zh + zt), q)))
+    z_peers = [(d, (at(y, lax.rem(z + 4 * d, 16)), q)) for d in range(1, 4)]
+    c_peers = []
+    for dq in range(8):
+        for dh in range(2):
+            if dq or dh:
+                qt = lax.rem(q + dq, 8)
+                ht = 1 - half if dh else half
+                c_peers.append((2 * dq + dh, qt, ht, (at(y, 4 * zh + 2 * ht + kb), qt)))
     k_peers = []
     for dy in range(4):
         for dk in range(2):
@@ -57,27 +74,23 @@
                 yt = lax.rem(y + dy, 4)
                 kt = yt * 2 + (1 - kb if dk else kb)
                 k_peers.append((2 * dy + dk, kt, (at(yt, zpair if dk else z), q)))
-    t_peers = []
-    for d in range(1, 8):
-        zt = lax.rem(z + 2 * d, 16)
-        t_peers.append((d, lax.div(zt, 2), (at(y, zt), q)))
-    q_peers = [(d, lax.rem(q + d, 8), (s, lax.rem(q + d, 8))) for d in range(1, 8)]
-    odd_z = [(at(y, lax.rem(zpair + 2 * d, 16)), q) for d in range(1, 8)]
-
-    barrier = pltpu.get_barrier_semaphore()
-    for peer in [p[2] for p in k_peers + t_peers + q_peers] + odd_z:
-        pl.semaphore_signal(barrier, inc=1, device_id=peer, device_id_type=pl.DeviceIdType.MESH)
+    rest = [(at(y, 4 * lax.rem(zh + i, 4) + lax.rem(zl + j, 4)), q) for i in range(1, 4) for j in range(1, 4)]
 
     kcol = pl.ds(pl.multiple_of(k * 128, 128), 128)
     fcol = pl.ds(pl.multiple_of(k * 256, 256), 256)
     loads = [
         (wg_h, wg_v), (wu_h, wu_v), (wd_h, wd_v), (q_h, q_v), (k_h, k_v), (v_h, v_v),
         (nk_h.at[:, :, kcol], nk_v), (nv_h.at[:, :, kcol], nv_v),
-        (resid_h.at[:, :, fcol], res_v), (gain_h, gain_v),
+        (resid_h.at[pl.ds(2 * half, 2), :, fcol], res_v), (gain_h, gain_v),
     ]
     loads = [pltpu.make_async_copy(a, b, lsem.at[i]) for i, (a, b) in enumerate(loads)]
     for c in loads:
         c.start()
+
+    barrier = pltpu.get_barrier_semaphore()
+    greeted = [p[-1] for p in a_peers + z_peers + c_peers if p is not c_peers[0]] + rest
+    for peer in greeted:
+        pl.semaphore_signal(barrier, inc=1, device_id=peer, device_id_type=pl.DeviceIdType.MESH)
 
     def remote(src, dst, ssem, rsem, peer):
         return pltpu.make_async_remote_copy(
@@ -120,7 +133,7 @@
 
     def stats(top, tot):
         tile = jnp.zeros((8, 128), F32)
-        for i in range(8):
+        for i in range(4):
             tile = jnp.where(lane == i, top[8 * i:8 * i + 8], tile)
             tile = jnp.where(lane == 48 + i, tot[8 * i:8 * i + 8], tile)
         return tile
@@ -141,12 +154,13 @@
         w = jnp.where(mask, jnp.exp(sc - top), 0.0).astype(BF16)
         tot = jnp.sum(w.astype(F32), axis=1, keepdims=True)
         acc = jnp.dot(w, vals, preferred_element_type=F32).astype(BF16)
-        pa[kv, 0:8] = acc.reshape(8, 8, 128)
-        pa[kv, 8] = split3(stats(top, tot))
-
-    pl.semaphore_wait(barrier, 28)
-
-    ca = send([remote(pa.at[kt], ra.at[d], a_s.at[d], a_r.at[d], peer) for d, kt, peer in k_peers])
+        for h in range(2):
+            pa[kv, h, 0:4] = acc[32 * h:32 * h + 32].reshape(4, 8, 128)
+            pa[kv, h, 4] = split3(stats(top[32 * h:32 * h + 32], tot[32 * h:32 * h + 32]))
+
+    pl.semaphore_wait(barrier, len(greeted))
+
+    ca = send([remote(pa.at[kt, ht], ra.at[d], a_s.at[d], a_r.at[d], peer) for d, kt, ht, peer in a_peers])
 
     for j in range(8):
         zt = 2 * j + zhi
@@ -164,17 +178,17 @@
         c.wait()
     qf = jnp.concatenate(
         [
-            q_v[tt, :, pl.ds(pl.multiple_of(k * 256 + 128 * gg, 128), 128)].astype(F32)
-            for tt in range(4) for gg in range(2)
+            q_v[2 * half + tt, :, pl.ds(pl.multiple_of(k * 256 + 128 * gg, 128), 128)].astype(F32)
+            for tt in range(2) for gg in range(2)
         ],
         axis=0,
     ).astype(BF16)
     nk = nk_v[...].astype(F32).reshape(32, 128).astype(BF16)
     nv = nv_v[...].astype(F32).reshape(32, 128).astype(BF16)
     fs = lax.dot_general(qf, nk, NT, preferred_element_type=F32) * SCALE
-    frow = lax.broadcasted_iota(jnp.int32, (64, 32), 0)
-    fcl = lax.broadcasted_iota(jnp.int32, (64, 32), 1)
-    fmask = ((fcl & 7) == (frow & 7)) & (lax.shift_right_logical(fcl, 3) <= lax.shift_right_logical(frow, 4))
+    frow = lax.broadcasted_iota(jnp.int32, (32, 32), 0)
+    fcl = lax.broadcasted_iota(jnp.int32, (32, 32), 1)
+    fmask = ((fcl & 7) == (frow & 7)) & (lax.shift_right_logical(fcl, 3) <= lax.shift_right_logical(frow, 4) + 2 * half)
     fs = jnp.where(fmask, fs, NEG_FILL)
     ftop = jnp.max(fs, axis=1, keepdims=True)
     fw = jnp.where(fmask, jnp.exp(fs - ftop), 0.0).astype(BF16)
@@ -188,30 +202,31 @@
         total = sum(pltpu.roll(f, 48, 1) * v for f, v in zip(fac, parts))
         return peak, fac, total
 
-    ra[0] = pa[k]
+    ra[0] = pa[k, half]
     for c in ca:
         c.wait_recv()
-    peak, fac, total = merge([join3(ra[d, 8].astype(F32)) for d in range(8)])
-    for i in range(8):
-        pb[i] = sum(fac[d][:, i:i + 1] * ra[d, i].astype(F32) for d in range(8)).astype(BF16)
-    pb[8] = split3(jnp.where(lane < 8, peak, jnp.where((lane >= 48) & (lane < 56), total, 0.0)))
-
-    cb = send([remote(pb, rb.at[tg], b_s.at[d], b_r.at[d], peer) for d, _, peer in t_peers])
-    rb[tg] = pb[...]
+    peak, fac, total = merge([join3(ra[d, 4].astype(F32)) for d in range(16)])
+    for i in range(4):
+        pb[i] = sum(fac[d][:, i:i + 1] * ra[d, i].astype(F32) for d in range(16)).astype(BF16)
+    pb[4] = split3(jnp.where(lane < 4, peak, jnp.where((lane >= 48) & (lane < 52), total, 0.0)))
+
+    cb = send([remote(pb, rb.at[zh], b_s.at[d], b_r.at[d], peer) for d, peer in z_peers])
+    rb[zh] = pb[...]
     for c in cb:
         c.wait_recv()
-    _, fac, total = merge([join3(rb[d, 8].astype(F32)) for d in range(8)] + [fstat])
+    _, fac, total = merge([join3(rb[d, 4].astype(F32)) for d in range(4)] + [fstat])
     inverse = pltpu.roll(total, 80, 1)
-    for i in range(8):
-        acc = sum(fac[d][:, i:i + 1] * rb[d, i].astype(F32) for d in range(8))
-        acc = acc + fac[8][:, i:i + 1] * facc[8 * i:8 * i + 8]
+    for i in range(4):
+        acc = sum(fac[d][:, i:i + 1] * rb[d, i].astype(F32) for d in range(4))
+        acc = acc + fac[4][:, i:i + 1] * facc[8 * i:8 * i + 8]
         attn = (acc / inverse[:, i:i + 1]).astype(BF16).astype(F32)
         tt, gg = i // 2, i % 2
-        x_v[q, tt, :, 128 * gg:128 * gg + 128] = (
+        x_v[q, 2 * half + tt, :, 128 * gg:128 * gg + 128] = (
             res_v[tt, :, 128 * gg:128 * gg + 128].astype(F32) + attn
         ).astype(BF16)
 
-    cd = send([remote(x_v.at[q], x_v.at[q], d_s.at[d], d_r.at[d], peer) for d, _, peer in q_peers])
+    mine = x_v.at[q, pl.ds(2 * half, 2)]
+    cd = send([remote(mine, mine, d_s.at[d], d_r.at[d], peer) for d, _, _, peer in c_peers])
     for f8 in range(8):
         copy = remote(ws.at[f8], wr.at[f8], ws_s.at[f8], ws_r.at[f8], (s, q))
 
@@ -249,20 +264,21 @@
     down = lax.dot_general(
         hh[...].reshape(256, 128), wr[:, :, 256:384].reshape(256, 128), NT, preferred_element_type=F32
     )
-    dd[...] = down.astype(BF16).reshape(8, 32, 256)
-    cg = send([remote(dd.at[qt], rd.at[d], g_s.at[d], g_r.at[d], peer) for d, qt, peer in q_peers])
-    rd[0] = dd[q]
+    dd[...] = down.astype(BF16).reshape(8, 2, 16, 256)
+    cg = send([remote(dd.at[qt, ht], rd.at[d], g_s.at[d], g_r.at[d], peer) for d, qt, ht, peer in c_peers])
+    rd[0] = dd[q, half]
     for c in cg:
         c.wait_recv()
     ee[...] = jnp.sum(rd[...].astype(F32), axis=0).astype(BF16)
-    ch = send([remote(ee, re.at[tg], h_s.at[d], h_r.at[d], peer) for d, _, peer in t_peers])
-    re[tg] = ee[...]
+    ch = send([remote(ee, re.at[zh], h_s.at[d], h_r.at[d], peer) for d, peer in z_peers])
+    re[zh] = ee[...]
     for c in ch:
         c.wait_recv()
-    final = x_v[q].astype(F32) + jnp.sum(re[...].astype(F32), axis=0).reshape(4, 8, 256)
-    out[:, :, fcol] = final.astype(BF16)
-
-    ci = send([remote(out.at[:, :, fcol], out.at[:, :, fcol], c_s.at[d], c_r.at[d], peer) for d, _, peer in k_peers])
+    final = mine[...].astype(F32) + jnp.sum(re[...].astype(F32), axis=0).reshape(2, 8, 256)
+    piece = out.at[pl.ds(2 * half, 2), :, fcol]
+    piece[...] = final.astype(BF16)
+
+    ci = send([remote(piece, piece, c_s.at[d], c_r.at[d], peer) for d, _, _, peer in a_peers])
     for c in ci:
         c.wait_recv()
 
@@ -282,8 +298,8 @@
     dma = lambda n: pltpu.SemaphoreType.DMA((n,))
     vm = pltpu.VMEM
     sems = []
-    for _ in range(9):
-        sems += [dma(8), dma(8)]
+    for n in (8, 16, 4, 16, 16, 8, 8, 16, 4):
+        sems += [dma(n), dma(n)]
     return pl.pallas_call(
         kernel,
         out_shape=jax.ShapeDtypeStruct((4, 8, 2048), BF16),
@@ -291,16 +307,16 @@
         out_specs=pl.BlockSpec(memory_space=pltpu.VMEM),
         scratch_shapes=[
             vm((4, 8, 2048), BF16), vm((4, 8, 128), BF16), vm((4, 8, 128), BF16),
-            vm((8, 32, 1024), BF16), vm((8, 32, 1024), BF16), vm((4, 8, 256), BF16), vm((2048,), BF16),
+            vm((8, 32, 1024), BF16), vm((8, 32, 1024), BF16), vm((2, 8, 256), BF16), vm((2048,), BF16),
             vm((32, 768), BF16), vm((32, 768), BF16), vm((32, 768), BF16),
             vm((8, 32, 384), BF16), vm((8, 32, 384), BF16),
-            vm((8, 9, 8, 128), BF16), vm((8, 9, 8, 128), BF16),
-            vm((9, 8, 128), BF16), vm((8, 9, 8, 128), BF16),
+            vm((8, 2, 5, 8, 128), BF16), vm((16, 5, 8, 128), BF16),
+            vm((5, 8, 128), BF16), vm((4, 5, 8, 128), BF16),
             vm((8, 4, 8, 256), BF16),
             vm((8, 32, 256), BF16), vm((8, 32, 256), BF16),
             vm((8, 32, 128), BF16),
-            vm((8, 32, 256), BF16), vm((8, 32, 256), BF16),
-            vm((32, 256), BF16), vm((8, 32, 256), BF16),
+            vm((8, 2, 16, 256), BF16), vm((16, 16, 256), BF16),
+            vm((16, 256), BF16), vm((4, 16, 256), BF16),
             dma(10),
         ] + sems,
         compiler_params=pltpu.CompilerParams(

time: 74.7 us -> 73.3 us (0.981)
  the two profiles are of different devices: /device:TPU:24 before, /device:TPU:1 now
where the time goes in v4:
time: 73.3 us; the launch traced here: 73.2 us
  Pallas kernels  71.6 us (98%)
  local copies, waits for them, and re-layouts  1.57 us (2%)
    pallas_call x1, Pallas kernels, step(): pl.pallas_call(kernel, out_shape=jax.ShapeDtypeStruct((4, 8, 2048), BF16)...  71.6 us
    unnamed x1, local copies, waits for them, and re-layouts  1.57 us

profile of v4, /device:TPU:1, one launch (start us, length us, event | category | flops | bytes accessed | tf_op | source)
XLA Modules:
  0.0 73.2 jit_solution(2722222287172302207)
XLA Ops:
  0.0 71.6 %shard_map.109 = bf16[4,8,2048]{2,1,0:T(8,128)(2,1)} custom-call(bf16[4,8,2048]{2,1,0:T(8,128)(2,1)} %q_h.1, bf16[4,8,1024]{2,1,0:T(8,128)(2,1)} %nk_h.1, bf16[4,8,1024]{2,1,0:T(8,128)(2,1)} %nv_h.1, bf16[8,32,1024]{2,1,0:T(8,128)(2,1)} %k_h.1, bf16[8,32,1024]{2,1,0:T(8,128)(2,1)} %v_h.1, s32[8]{0:T(128)} %len_s.1, bf16[4,8,2048]{2,1,0:T(8,128)(2,1)} %resid_h.1, ...), custom_call_target="tpu_custom_call" | custom-call | tf_op jit(solution)/shard_map/pallas_call | solution.py:303
  71.6 1.6 %copy.13 = bf16[4,8,2048]{2,1,0:T(8,128)(2,1)} copy(bf16[4,8,2048]{2,1,0:T(8,128)(2,1)} %shard_map.109) | data formatting | bytes 262144

commit v5 on v4

--- a/solution.py
+++ b/solution.py
@@ -32,9 +32,9 @@
     q_h, nk_h, nv_h, k_h, v_h, len_s, resid_h, gain_h, wg_h, wu_h, wd_h,
     out,
     q_v, nk_v, nv_v, k_v, v_v, res_v, gain_v, wg_v, wu_v, wd_v,
-    ws, wr, pa, ra, pb, rb, x_v, pp, rp, hh, dd, rd, ee, re,
+    ws, wr, us, ur, pa, ra, pb, rb, x_v, pp, rp, hh, dd, rd, ee, re,
     lsem,
-    ws_s, ws_r, a_s, a_r, b_s, b_r, c_s, c_r, d_s, d_r, e_s, e_r, f_s, f_r, g_s, g_r, h_s, h_r,
+    ws_s, ws_r, us_s, us_r, a_s, a_r, b_s, b_r, c_s, c_r, d_s, d_r, e_s, e_r, f_s, f_r, g_s, g_r, h_s, h_r,
 ):
     s = lax.axis_index("seq")
     q = lax.axis_index("req")
@@ -59,7 +59,8 @@
                 yt, zt = lax.rem(y + dy, 4), lax.rem(zl + dz, 4)
                 kt, ht = yt * 2 + lax.rem(zt, 2), lax.div(zt, 2)
                 a_peers.append((4 * dy + dz, kt, ht, (at(yt, 4 * zh + zt), q)))
-    z_peers = [(d, (at(y, lax.rem(z + 4 * d, 16)), q)) for d in range(1, 4)]
+    a_peers.sort(key=lambda p: -(min(p[0] // 4, 4 - p[0] // 4) * 2 + min(p[0] % 4, 2)))
+    z_peers = [(d, (at(y, lax.rem(z + 4 * d, 16)), q)) for d in (2, 1, 3)]
     c_peers = []
     for dq in range(8):
         for dh in range(2):
@@ -67,6 +68,7 @@
                 qt = lax.rem(q + dq, 8)
                 ht = 1 - half if dh else half
                 c_peers.append((2 * dq + dh, qt, ht, (at(y, 4 * zh + 2 * ht + kb), qt)))
+    c_peers.sort(key=lambda p: -(min(p[0] // 4, 4 - p[0] // 4) + 2 * (p[0] % 2)))
     k_peers = []
     for dy in range(4):
         for dk in range(2):
@@ -74,6 +76,7 @@
                 yt = lax.rem(y + dy, 4)
                 kt = yt * 2 + (1 - kb if dk else kb)
                 k_peers.append((2 * dy + dk, kt, (at(yt, zpair if dk else z), q)))
+    k_peers.sort(key=lambda p: -(min(p[0] // 2, 4 - p[0] // 2) + p[0] % 2))
     rest = [(at(y, 4 * lax.rem(zh + i, 4) + lax.rem(zl + j, 4)), q) for i in range(1, 4) for j in range(1, 4)]
 
     kcol = pl.ds(pl.multiple_of(k * 128, 128), 128)
@@ -88,7 +91,8 @@
         c.start()
 
     barrier = pltpu.get_barrier_semaphore()
-    greeted = [p[-1] for p in a_peers + z_peers + c_peers if p is not c_peers[0]] + rest
+    same = [p for p in c_peers if p[0] == 1][0]
+    greeted = [p[-1] for p in a_peers + z_peers + c_peers if p is not same] + rest
     for peer in greeted:
         pl.semaphore_signal(barrier, inc=1, device_id=peer, device_id_type=pl.DeviceIdType.MESH)
 
@@ -105,21 +109,6 @@
             c.start()
         sent.extend(copies)
         return copies
-
-    for c in loads[:3]:
-        c.wait()
-    whole = [wg_v[...].astype(F32), wu_v[...].astype(F32), wd_v[...].astype(F32)]
-    keep = lax.broadcasted_iota(jnp.int32, (32, 128), 1) < 96
-    for j in range(8):
-        base, off = (96 * j) // 128 * 128, (96 * j) % 128
-        for i, w in enumerate(whole):
-            if off + 96 <= 128:
-                piece = w[:, base:base + 128]
-                if off:
-                    piece = pltpu.roll(piece, 128 - off, 1)
-            else:
-                piece = pltpu.roll(w[:, base:base + 256], 256 - off, 1)[:, :128]
-            ws[j, :, 128 * i:128 * i + 128] = jnp.where(keep, piece, 0.0).astype(BF16)
 
     for c in loads[3:6]:
         c.wait()
@@ -162,17 +151,44 @@
 
     ca = send([remote(pa.at[kt, ht], ra.at[d], a_s.at[d], a_r.at[d], peer) for d, kt, ht, peer in a_peers])
 
+    for c in loads[:3]:
+        c.wait()
+    whole = [wg_v[...].astype(F32), wu_v[...].astype(F32), wd_v[...].astype(F32)]
+    keep = lax.broadcasted_iota(jnp.int32, (32, 128), 1) < 96
     for j in range(8):
-        zt = 2 * j + zhi
-        copy = remote(ws.at[j], wr.at[zlo], ws_s.at[j], ws_r.at[zlo], (at(y, zt), q))
-
-        @pl.when(zt != z)
-        def _():
-            copy.start()
-
-        @pl.when(zt == z)
-        def _():
-            wr[zlo] = ws[j]
+        base, off = (96 * j) // 128 * 128, (96 * j) % 128
+        for i, w in enumerate(whole):
+            if off + 96 <= 128:
+                piece = w[:, base:base + 128]
+                if off:
+                    piece = pltpu.roll(piece, 128 - off, 1)
+            else:
+                piece = pltpu.roll(w[:, base:base + 256], 256 - off, 1)[:, :128]
+            part = jnp.where(keep, piece, 0.0).astype(BF16)
+            if i < 2:
+                ws[j, :, 128 * i:128 * i + 128] = part
+            else:
+                us[j] = part
+
+    def weights(src, dst, ssem, rsem, action):
+        for j in range(8):
+            zt = 2 * j + zhi
+            copy = remote(src.at[j], dst.at[zlo], ssem.at[j], rsem.at[zlo], (at(y, zt), q))
+            if action == "wait":
+                copy = remote(src.at[j], dst.at[j], ssem.at[j], rsem.at[j], (s, q))
+
+            @pl.when(8 * kb + j != z if action == "wait" else zt != z)
+            def _():
+                {"start": copy.start, "wait": copy.wait_recv, "end": copy.wait_send}[action]()
+
+            if action == "start":
+
+                @pl.when(zt == z)
+                def _():
+                    dst[zlo] = src[j]
+
+    gate_up = (ws, wr, ws_s, ws_r)
+    down_w = (us, ur, us_s, us_r)
 
     for c in loads[6:]:
         c.wait()
@@ -211,6 +227,7 @@
     pb[4] = split3(jnp.where(lane < 4, peak, jnp.where((lane >= 48) & (lane < 52), total, 0.0)))
 
     cb = send([remote(pb, rb.at[zh], b_s.at[d], b_r.at[d], peer) for d, peer in z_peers])
+    weights(*gate_up, "start")
     rb[zh] = pb[...]
     for c in cb:
         c.wait_recv()
@@ -227,19 +244,15 @@
 
     mine = x_v.at[q, pl.ds(2 * half, 2)]
     cd = send([remote(mine, mine, d_s.at[d], d_r.at[d], peer) for d, _, _, peer in c_peers])
-    for f8 in range(8):
-        copy = remote(ws.at[f8], wr.at[f8], ws_s.at[f8], ws_r.at[f8], (s, q))
-
-        @pl.when(8 * kb + f8 != z)
-        def _():
-            copy.wait_recv()
+    weights(*down_w, "start")
     for c in cd:
         c.wait_recv()
+    weights(*gate_up, "wait")
 
     xf = x_v[...].astype(F32).reshape(256, 256)
     square = jnp.sum(xf * xf, axis=1, keepdims=True)
     xg = (xf * gain_v[fcol].astype(F32).reshape(1, 256)).astype(BF16)
-    gu = jnp.dot(xg, wr[:, :, 0:256].reshape(256, 256), preferred_element_type=F32)
+    gu = jnp.dot(xg, wr[...].reshape(256, 256), preferred_element_type=F32)
     hi = square.astype(BF16).astype(F32)
     lane2 = lax.broadcasted_iota(jnp.int32, (256, 256), 1)
     gu = jnp.where(lane2 == 96, hi, jnp.where(lane2 == 97, square - hi, gu))
@@ -261,8 +274,9 @@
     for c in cf:
         c.wait_recv()
 
+    weights(*down_w, "wait")
     down = lax.dot_general(
-        hh[...].reshape(256, 128), wr[:, :, 256:384].reshape(256, 128), NT, preferred_element_type=F32
+        hh[...].reshape(256, 128), ur[...].reshape(256, 128), NT, preferred_element_type=F32
     )
     dd[...] = down.astype(BF16).reshape(8, 2, 16, 256)
     cg = send([remote(dd.at[qt, ht], rd.at[d], g_s.at[d], g_r.at[d], peer) for d, qt, ht, peer in c_peers])
@@ -284,13 +298,8 @@
 
     for c in sent:
         c.wait_send()
-    for j in range(8):
-        zt = 2 * j + zhi
-        copy = remote(ws.at[j], wr.at[zlo], ws_s.at[j], ws_r.at[zlo], (at(y, zt), q))
-
-        @pl.when(zt != z)
-        def _():
-            copy.wait_send()
+    weights(*gate_up, "end")
+    weights(*down_w, "end")
 
 
 def step(q, nk, nv, kc, vc, cache_len, resid, gain, w_gate, w_up, w_down):
@@ -298,7 +307,7 @@
     dma = lambda n: pltpu.SemaphoreType.DMA((n,))
     vm = pltpu.VMEM
     sems = []
-    for n in (8, 16, 4, 16, 16, 8, 8, 16, 4):
+    for n in (8, 8, 16, 4, 16, 16, 8, 8, 16, 4):
         sems += [dma(n), dma(n)]
     return pl.pallas_call(
         kernel,
@@ -309,7 +318,7 @@
             vm((4, 8, 2048), BF16), vm((4, 8, 128), BF16), vm((4, 8, 128), BF16),
             vm((8, 32, 1024), BF16), vm((8, 32, 1024), BF16), vm((2, 8, 256), BF16), vm((2048,), BF16),
             vm((32, 768), BF16), vm((32, 768), BF16), vm((32, 768), BF16),
-            vm((8, 32, 384), BF16), vm((8, 32, 384), BF16),
+            vm((8, 32, 256), BF16), vm((8, 32, 256), BF16), vm((8, 32, 128), BF16), vm((8, 32, 128), BF16),
             vm((8, 2, 5, 8, 128), BF16), vm((16, 5, 8, 128), BF16),
             vm((5, 8, 128), BF16), vm((4, 5, 8, 128), BF16),
             vm((8, 4, 8, 256), BF16),

time: 73.3 us -> 66.6 us (0.909)
  the two profiles are of different devices: /device:TPU:1 before, /device:TPU:24 now
where the time goes in v5:
time: 66.6 us; the launch traced here: 65.5 us
  Pallas kernels  64 us (96%)
  local copies, waits for them, and re-layouts  1.57 us (2%)
    pallas_call x1, Pallas kernels, step(): pl.pallas_call(kernel, out_shape=jax.ShapeDtypeStruct((4, 8, 2048), BF16)...  64 us
    unnamed x1, local copies, waits for them, and re-layouts  1.57 us

profile of v5, /device:TPU:24, one launch (start us, length us, event | category | flops | bytes accessed | tf_op | source)
XLA Modules:
  0.0 65.5 jit_solution(6324625835409636104)
XLA Ops:
  0.0 64.0 %shard_map.109 = bf16[4,8,2048]{2,1,0:T(8,128)(2,1)} custom-call(bf16[4,8,2048]{2,1,0:T(8,128)(2,1)} %q_h.1, bf16[4,8,1024]{2,1,0:T(8,128)(2,1)} %nk_h.1, bf16[4,8,1024]{2,1,0:T(8,128)(2,1)} %nv_h.1, bf16[8,32,1024]{2,1,0:T(8,128)(2,1)} %k_h.1, bf16[8,32,1024]{2,1,0:T(8,128)(2,1)} %v_h.1, s32[8]{0:T(128)} %len_s.1, bf16[4,8,2048]{2,1,0:T(8,128)(2,1)} %resid_h.1, ...), custom_call_target="tpu_custom_call" | custom-call | tf_op jit(solution)/shard_map/pallas_call | solution.py:312
  64.0 1.6 %copy.13 = bf16[4,8,2048]{2,1,0:T(8,128)(2,1)} copy(bf16[4,8,2048]{2,1,0:T(8,128)(2,1)} %shard_map.109) | data formatting | bytes 262144

commit v6 on v5

--- a/solution.py
+++ b/solution.py
@@ -329,9 +329,9 @@
             dma(10),
         ] + sems,
         compiler_params=pltpu.CompilerParams(
-            collective_id=0, has_side_effects=True, vmem_limit_bytes=60 * 1024 * 1024
+            collective_id=0, has_side_effects=True, vmem_limit_bytes=16 * 1024 * 1024
         ),
-    )(q, nk, nv, kc, vc, cache_len, resid, gain, w_gate, w_up, w_down.T)
+    )(*[pltpu.with_memory_space_constraint(a, pltpu.HBM) for a in (q, nk, nv, kc, vc, cache_len, resid, gain, w_gate, w_up, w_down.T)])
 
 
 def solution(mesh):

time: 66.6 us -> 65.1 us (0.977)
  local copies, waits for them, and re-layouts: 1.57 us -> 0.66 us
  Pallas kernels: 64 us -> 63.3 us
    unnamed x1, local copies, waits for them, and re-layouts: 1.57 us -> 0.66 us
where the time goes in v6:
time: 65.1 us; the launch traced here: 64 us
  Pallas kernels  63.3 us (97%)
  local copies, waits for them, and re-layouts  0.66 us (1%)
    pallas_call x1, Pallas kernels, step(): pl.pallas_call(kernel, out_shape=jax.ShapeDtypeStruct((4, 8, 2048), BF16)...  63.3 us

profile of v6, /device:TPU:24, one launch (start us, length us, event | category | flops | bytes accessed | tf_op | source)
XLA Modules:
  0.0 64.0 jit_solution(16873236589641881544)
XLA Ops:
  0.0 63.3 %shard_map.109 = bf16[4,8,2048]{2,1,0:T(8,128)(2,1)S(1)} custom-call(bf16[4,8,2048]{2,1,0:T(8,128)(2,1)} %q_h.1, bf16[4,8,1024]{2,1,0:T(8,128)(2,1)} %nk_h.1, bf16[4,8,1024]{2,1,0:T(8,128)(2,1)} %nv_h.1, bf16[8,32,1024]{2,1,0:T(8,128)(2,1)} %k_h.1, bf16[8,32,1024]{2,1,0:T(8,128)(2,1)} %v_h.1, s32[8]{0:T(128)} %len_s.1, bf16[4,8,2048]{2,1,0:T(8,128)(2,1)} %resid_h.1, ...), custom_call_target="tpu_custom_call" | custom-call | tf_op jit(solution)/shard_map/pallas_call | solution.py:312
  63.3 0.7 %copy.13 = bf16[4,8,2048]{2,1,0:T(8,128)(2,1)} copy(bf16[4,8,2048]{2,1,0:T(8,128)(2,1)S(1)} %shard_map.109) | data formatting | bytes 262144

commit v7 on v6

--- a/solution.py
+++ b/solution.py
@@ -33,7 +33,7 @@
     out,
     q_v, nk_v, nv_v, k_v, v_v, res_v, gain_v, wg_v, wu_v, wd_v,
     ws, wr, us, ur, pa, ra, pb, rb, x_v, pp, rp, hh, dd, rd, ee, re,
-    lsem,
+    lsem, near1, near2,
     ws_s, ws_r, us_s, us_r, a_s, a_r, b_s, b_r, c_s, c_r, d_s, d_r, e_s, e_r, f_s, f_r, g_s, g_r, h_s, h_r,
 ):
     s = lax.axis_index("seq")
@@ -77,7 +77,7 @@
                 kt = yt * 2 + (1 - kb if dk else kb)
                 k_peers.append((2 * dy + dk, kt, (at(yt, zpair if dk else z), q)))
     k_peers.sort(key=lambda p: -(min(p[0] // 2, 4 - p[0] // 2) + p[0] % 2))
-    rest = [(at(y, 4 * lax.rem(zh + i, 4) + lax.rem(zl + j, 4)), q) for i in range(1, 4) for j in range(1, 4)]
+    steps_z = [p[-1] for p in z_peers if p[0] != 2]
 
     kcol = pl.ds(pl.multiple_of(k * 128, 128), 128)
     fcol = pl.ds(pl.multiple_of(k * 256, 256), 256)
@@ -92,7 +92,7 @@
 
     barrier = pltpu.get_barrier_semaphore()
     same = [p for p in c_peers if p[0] == 1][0]
-    greeted = [p[-1] for p in a_peers + z_peers + c_peers if p is not same] + rest
+    greeted = [p[-1] for p in a_peers + c_peers if p is not same] + steps_z
     for peer in greeted:
         pl.semaphore_signal(barrier, inc=1, device_id=peer, device_id_type=pl.DeviceIdType.MESH)
 
@@ -101,6 +101,10 @@
             src_ref=src, dst_ref=dst, send_sem=ssem, recv_sem=rsem,
             device_id=peer, device_id_type=pl.DeviceIdType.MESH,
         )
+
+    def tell(sem):
+        for peer in steps_z:
+            pl.semaphore_signal(sem, inc=1, device_id=peer, device_id_type=pl.DeviceIdType.MESH)
 
     sent = []
 
@@ -151,6 +155,8 @@
 
     ca = send([remote(pa.at[kt, ht], ra.at[d], a_s.at[d], a_r.at[d], peer) for d, kt, ht, peer in a_peers])
 
+    tell(near1)
+
     for c in loads[:3]:
         c.wait()
     whole = [wg_v[...].astype(F32), wu_v[...].astype(F32), wd_v[...].astype(F32)]
@@ -172,8 +178,9 @@
 
     def weights(src, dst, ssem, rsem, action):
         for j in range(8):
-            zt = 2 * j + zhi
-            copy = remote(src.at[j], dst.at[zlo], ssem.at[j], rsem.at[zlo], (at(y, zt), q))
+            block = lax.rem(lax.div(z, 2) + (4, 3, 5, 2, 6, 1, 7, 0)[j], 8)
+            zt = 2 * block + zhi
+            copy = remote(src.at[block], dst.at[zlo], ssem.at[j], rsem.at[zlo], (at(y, zt), q))
             if action == "wait":
                 copy = remote(src.at[j], dst.at[j], ssem.at[j], rsem.at[j], (s, q))
 
@@ -185,7 +192,7 @@
 
                 @pl.when(zt == z)
                 def _():
-                    dst[zlo] = src[j]
+                    dst[zlo] = src[block]
 
     gate_up = (ws, wr, ws_s, ws_r)
     down_w = (us, ur, us_s, us_r)
@@ -218,6 +225,8 @@
         total = sum(pltpu.roll(f, 48, 1) * v for f, v in zip(fac, parts))
         return peak, fac, total
 
+    pl.semaphore_wait(near1, 2)
+    tell(near2)
     ra[0] = pa[k, half]
     for c in ca:
         c.wait_recv()
@@ -227,6 +236,7 @@
     pb[4] = split3(jnp.where(lane < 4, peak, jnp.where((lane >= 48) & (lane < 52), total, 0.0)))
 
     cb = send([remote(pb, rb.at[zh], b_s.at[d], b_r.at[d], peer) for d, peer in z_peers])
+    pl.semaphore_wait(near2, 2)
     weights(*gate_up, "start")
     rb[zh] = pb[...]
     for c in cb:
@@ -326,7 +336,7 @@
             vm((8, 32, 128), BF16),
             vm((8, 2, 16, 256), BF16), vm((16, 16, 256), BF16),
             vm((16, 256), BF16), vm((4, 16, 256), BF16),
-            dma(10),
+            dma(10), pltpu.SemaphoreType.REGULAR, pltpu.SemaphoreType.REGULAR,
         ] + sems,
         compiler_params=pltpu.CompilerParams(
             collective_id=0, has_side_effects=True, vmem_limit_bytes=16 * 1024 * 1024

time: 65.1 us -> 64.7 us (level)
  no operation moved by 1% of the time
where the time goes in v7:
time: 64.7 us; the launch traced here: 63.8 us
  Pallas kernels  63.1 us (98%)
  local copies, waits for them, and re-layouts  0.66 us (1%)
    pallas_call x1, Pallas kernels, step(): pl.pallas_call(kernel, out_shape=jax.ShapeDtypeStruct((4, 8, 2048), BF16)...  63.1 us

profile of v7, /device:TPU:24, one launch (start us, length us, event | category | flops | bytes accessed | tf_op | source)
XLA Modules:
  0.0 63.8 jit_solution(8599039399641563831)
XLA Ops:
  0.0 63.1 %shard_map.109 = bf16[4,8,2048]{2,1,0:T(8,128)(2,1)S(1)} custom-call(bf16[4,8,2048]{2,1,0:T(8,128)(2,1)} %q_h.1, bf16[4,8,1024]{2,1,0:T(8,128)(2,1)} %nk_h.1, bf16[4,8,1024]{2,1,0:T(8,128)(2,1)} %nv_h.1, bf16[8,32,1024]{2,1,0:T(8,128)(2,1)} %k_h.1, bf16[8,32,1024]{2,1,0:T(8,128)(2,1)} %v_h.1, s32[8]{0:T(128)} %len_s.1, bf16[4,8,2048]{2,1,0:T(8,128)(2,1)} %resid_h.1, ...), custom_call_target="tpu_custom_call" | custom-call | tf_op jit(solution)/shard_map/pallas_call | solution.py:322
  63.2 0.7 %copy.13 = bf16[4,8,2048]{2,1,0:T(8,128)(2,1)} copy(bf16[4,8,2048]{2,1,0:T(8,128)(2,1)S(1)} %shard_map.109) | data formatting | bytes 262144

commit v8 on v7

--- a/solution.py
+++ b/solution.py
@@ -294,8 +294,14 @@
     for c in cg:
         c.wait_recv()
     ee[...] = jnp.sum(rd[...].astype(F32), axis=0).astype(BF16)
+    older = list(sent)
+    sent.clear()
     ch = send([remote(ee, re.at[zh], h_s.at[d], h_r.at[d], peer) for d, peer in z_peers])
     re[zh] = ee[...]
+    for c in older:
+        c.wait_send()
+    weights(*gate_up, "end")
+    weights(*down_w, "end")
     for c in ch:
         c.wait_recv()
     final = mine[...].astype(F32) + jnp.sum(re[...].astype(F32), axis=0).reshape(2, 8, 256)
@@ -303,13 +309,10 @@
     piece[...] = final.astype(BF16)
 
     ci = send([remote(piece, piece, c_s.at[d], c_r.at[d], peer) for d, _, _, peer in a_peers])
-    for c in ci:
-        c.wait_recv()
-
     for c in sent:
         c.wait_send()
-    weights(*gate_up, "end")
-    weights(*down_w, "end")
+    for c in ci:
+        c.wait_recv()
 
 
 def step(q, nk, nv, kc, vc, cache_len, resid, gain, w_gate, w_up, w_down):

time: 64.7 us -> 64.5 us (level)
  no operation moved by 1% of the time
where the time goes in v8:
time: 64.5 us; the launch traced here: 63.7 us
  Pallas kernels  63 us (98%)
  local copies, waits for them, and re-layouts  0.66 us (1%)
    pallas_call x1, Pallas kernels, step(): pl.pallas_call(kernel, out_shape=jax.ShapeDtypeStruct((4, 8, 2048), BF16)...  63 us

profile of v8, /device:TPU:24, one launch (start us, length us, event | category | flops | bytes accessed | tf_op | source)
XLA Modules:
  0.0 63.7 jit_solution(18334595683217771771)
XLA Ops:
  0.0 63.0 %shard_map.109 = bf16[4,8,2048]{2,1,0:T(8,128)(2,1)S(1)} custom-call(bf16[4,8,2048]{2,1,0:T(8,128)(2,1)} %q_h.1, bf16[4,8,1024]{2,1,0:T(8,128)(2,1)} %nk_h.1, bf16[4,8,1024]{2,1,0:T(8,128)(2,1)} %nv_h.1, bf16[8,32,1024]{2,1,0:T(8,128)(2,1)} %k_h.1, bf16[8,32,1024]{2,1,0:T(8,128)(2,1)} %v_h.1, s32[8]{0:T(128)} %len_s.1, bf16[4,8,2048]{2,1,0:T(8,128)(2,1)} %resid_h.1, ...), custom_call_target="tpu_custom_call" | custom-call | tf_op jit(solution)/shard_map/pallas_call | solution.py:325
  63.0 0.7 %copy.13 = bf16[4,8,2048]{2,1,0:T(8,128)(2,1)} copy(bf16[4,8,2048]{2,1,0:T(8,128)(2,1)S(1)} %shard_map.109) | data formatting | bytes 262144
